TPU v7x, 512 devices: a whole 4x8x8 slice. The times are simulated.
512 devices in a mesh: dom: 64 (over z_lo, y, core), head: 8 (over z_hi, x).
Axes of the slice: x: 4, y: 8, z: 8 (z_hi: 2, z_lo: 4; z = z_hi * 4 + z_lo), core: 2. Of those that a mesh axis runs over, the one named last changes fastest.
Arguments:
- node_feats: bfloat16 [24576, 512], P('dom', 'head'), may hold values from -16 to 16
- tile_vals: bfloat16 [192, 4, 128, 128], P('dom'), may hold values from -0.375 to 0.375
- tile_counts: int32 [192], P('dom'), may hold values from 1 to 4
- tile_cols: int32 [192, 4], P('dom'), may hold values from 0 to 6
- send_rows: int32 [64, 4, 128], P('dom'), may hold values from 0 to 383, as said below
- w_msg: bfloat16 [512, 512], P(None, 'head'), may hold values from -0.25 to 0.25
- w_qkv: bfloat16 [3, 512, 512], P(None, None, 'head'), may hold values from -0.25 to 0.25
- w_out: bfloat16 [512, 512], P('head'), may hold values from -0.25 to 0.25
Outputs:
- updated: bfloat16 [24576, 512], P('dom', 'head')
Inputs may be any that keep to these rules, and one draw needn't show every extreme that they name: `send_rows`: local row indices within the sending partition. `tile_cols`: block c < 3 of a partition's row table is its own row block c; block 3 + j is the block of 128 rows received with offset index j.
All inputs are finite; a program needn't handle non-finite values.
Results may differ from a plain program's by a relative error of at most 0.012.
The roundings to bfloat16 on the way count: a program that leaves them out, or rounds other values in their place, can miss the bound.
Values may be sent and summed in bfloat16 or wider, within the bound.
No kernel may reach another device: no remote copies, remote signals or barrier semaphores. Data moves between devices by JAX's collectives and lax.ppermute only.
A program may use at most 64 MiB of HBM per device.

v0:
```python
import math

import jax
import jax.numpy as jnp
from jax import lax
from jax.experimental import pallas as pl
from jax.experimental.pallas import tpu as pltpu
from jax.sharding import Mesh
from jax.sharding import PartitionSpec as P


D = 512
H = 8
DH = D // H
REACH = 2
DOM = ("zl", "y", "c")
HEAD = ("zh", "x")
PARTS = (4, 8, 2, 2, 4)
CARRY = DH + 8
TILE_Q = 1024
TILE_K = 512
INTERPRET = False


def offsets(reach_count):
    return [
        position - reach_count if position < reach_count else position - reach_count + 1
        for position in range(2 * reach_count)
    ]


def passed_along(block, axis, distance):
    size = lax.axis_size(axis)
    return lax.ppermute(block, axis, [((i - distance) % size, i) for i in range(size)])


def sent_to_all(block, axis):
    size = lax.axis_size(axis)
    return lax.all_to_all(jnp.broadcast_to(block, (size,) + block.shape), axis, 0, 0)


def matmul(a, b, contract):
    return lax.dot_general(a, b, ((contract[0], contract[1]), ((), ())), preferred_element_type=jnp.float32)


def call(body, outs, scratch=(), smem=(), count=0, flops=0):
    specs = [
        pl.BlockSpec(memory_space=pltpu.SMEM if i in smem else pltpu.VMEM) for i in range(count)
    ]
    outputs = [jax.ShapeDtypeStruct(shape, dtype) for shape, dtype in outs]
    return pl.pallas_call(
        body,
        out_shape=outputs if len(outputs) > 1 else outputs[0],
        in_specs=specs,
        out_specs=[pl.BlockSpec(memory_space=pltpu.VMEM) for _ in outs]
        if len(outputs) > 1
        else pl.BlockSpec(memory_space=pltpu.VMEM),
        scratch_shapes=scratch,
        compiler_params=pltpu.CompilerParams(vmem_limit_bytes=48 * 1024 * 1024),
        cost_estimate=pl.CostEstimate(flops=flops, bytes_accessed=2000000, transcendentals=0),
        interpret=INTERPRET,
    )


def project_body(quad, weights, rows, q_out, kv_out, x_out, *chosen):
    per_z, per_x = quad.shape[1], quad.shape[0]
    for z in range(per_z):
        for x in range(per_x):
            at = (z * per_x + x) * DH
            x_out[at : at + DH, :] = quad[x, z]
    full = x_out[...]
    qkv = matmul(weights[...], full, ((1,), (0,)))
    query = qkv[:DH].astype(jnp.bfloat16).astype(jnp.float32) * (1.0 / math.sqrt(DH))
    for i in range(q_out.shape[0]):
        q_out[i] = query.astype(jnp.bfloat16)
    kv_out[...] = qkv[DH:].astype(jnp.bfloat16)
    count = full.shape[1]
    for j, out in enumerate(chosen):
        listed = rows[j : j + 1, :]
        spot = lax.broadcasted_iota(jnp.int32, (count, listed.shape[1]), 0) == listed
        out[...] = matmul(full, spot.astype(jnp.bfloat16), ((1,), (0,))).astype(jnp.bfloat16)


def three(value):
    high = value.astype(jnp.bfloat16).astype(jnp.float32)
    rest = value - high
    middle = rest.astype(jnp.bfloat16).astype(jnp.float32)
    return [high, middle, rest - middle]


def attend_body(q, kv, out, keys, values, queries, scores, weights, results):
    blocks, _, width = kv.shape
    for j in range(blocks):
        block = kv[j]
        at = slice(j * width, (j + 1) * width)
        keys[at, :] = block[:DH].T
        values[:DH, at] = block[DH:]
    values[DH:, :] = jnp.ones((CARRY - DH, blocks * width), jnp.bfloat16)
    count = q.shape[0]
    for i in range(count):
        queries[:, i * width : (i + 1) * width] = q[i]
    chunks = [slice(j * TILE_K, (j + 1) * TILE_K) for j in range(blocks * width // TILE_K)]

    def step(tile, carried):
        at = pl.multiple_of(tile * TILE_Q, TILE_Q)
        asked = queries[:, pl.ds(at, TILE_Q)]
        best = None
        for chunk in chunks:
            part = matmul(keys[chunk, :], asked, ((1,), (0,)))
            scores[chunk, :] = part
            high = part.reshape(TILE_K // 8, 8, TILE_Q).max(axis=0)
            best = high if best is None else jnp.maximum(best, high)
        top = best.max(axis=0, keepdims=True)
        for chunk in chunks:
            weights[chunk, :] = jnp.exp(scores[chunk, :] - top).astype(jnp.bfloat16)
        total = matmul(values[...], weights[...], ((1,), (0,)))
        rows = [total[:DH]] + three(top) + three(total[DH : DH + 1]) + [jnp.zeros((2, TILE_Q), jnp.float32)]
        results[:, pl.ds(at, TILE_Q)] = jnp.concatenate(rows, axis=0).astype(jnp.bfloat16)
        return carried

    lax.fori_loop(0, count * width // TILE_Q, step, 0)
    for i in range(count):
        out[i] = results[:, i * width : (i + 1) * width]


def combine_body(parts, w_out, out):
    count = parts.shape[0]
    tail = [parts[i, DH:, :].astype(jnp.float32) for i in range(count)]
    tops = [t[0:1] + t[1:2] + t[2:3] for t in tail]
    sums = [t[3:4] + t[4:5] + t[5:6] for t in tail]
    best = tops[0]
    for top in tops[1:]:
        best = jnp.maximum(best, top)
    total = jnp.zeros_like(best)
    value = jnp.zeros((DH, best.shape[1]), jnp.float32)
    for i in range(count):
        factor = jnp.exp(tops[i] - best)
        total = total + factor * sums[i]
        value = value + factor * parts[i, :DH, :].astype(jnp.float32)
    heads_out = (value / total).astype(jnp.bfloat16)
    for h in range(H):
        share = matmul(w_out[:, h * DH : (h + 1) * DH], heads_out, ((0,), (0,)))
        out[h] = share.astype(jnp.bfloat16)


def message_body(x, r0, r1, r2, r3, tiles, counts, cols, w_msg, own_x, out, table):
    own, slots, size, _ = tiles.shape
    for b in range(own):
        table[b] = x[:, b * size : (b + 1) * size]
    for j, received in enumerate((r0, r1, r2, r3)):
        table[own + j] = received[...]
    for r in range(own):
        total = jnp.zeros((D, size), jnp.float32)
        for t in range(slots):
            tile = tiles[r, t]
            tile = jnp.where(t < counts[r], tile, jnp.zeros_like(tile))
            total = total + matmul(table[cols[r, t]], tile, ((1,), (1,)))
        projected = matmul(w_msg[...], total.astype(jnp.bfloat16), ((1,), (0,)))
        at = slice(r * size, (r + 1) * size)
        out[:, at] = own_x[:, at].astype(jnp.float32) + jnp.maximum(projected, 0.0)


def local(node_feats, tile_vals, tile_counts, tile_cols, send_rows, w_msg, w_qkv, w_out):
    rows = node_feats.shape[0]
    bf16, f32 = jnp.bfloat16, jnp.float32
    listed = send_rows[0]
    directions, bound = listed.shape
    askers, givers = lax.axis_size("y"), lax.axis_size(("zl", "c"))
    keys, asked = givers * rows, askers * rows
    x_own = node_feats.T
    pair = lax.all_gather(x_own, "zh", axis=0, tiled=False)
    quad = sent_to_all(pair, "x")
    weights = jnp.swapaxes(w_qkv, 1, 2).reshape(3 * DH, D)
    q, kv, x_full, *chosen = call(
        project_body,
        [((askers, DH, rows), bf16), ((2 * DH, rows), bf16), ((D, rows), bf16)]
        + [((D, bound), bf16)] * directions,
        count=3,
        flops=2 * D * rows * (3 * DH + directions * bound),
    )(quad, weights, listed)
    queries = lax.all_to_all(q, "y", 0, 0)
    held = lax.all_gather(kv, ("zl", "c"), axis=0, tiled=False)
    parts = call(
        attend_body,
        [((askers, CARRY, rows), bf16)],
        scratch=[
            pltpu.VMEM((keys, DH), bf16),
            pltpu.VMEM((CARRY, keys), bf16),
            pltpu.VMEM((DH, asked), bf16),
            pltpu.VMEM((keys, TILE_Q), f32),
            pltpu.VMEM((keys, TILE_Q), bf16),
            pltpu.VMEM((CARRY, asked), bf16),
        ],
        count=2,
        flops=4 * DH * keys * asked,
    )(queries, held)
    parts = lax.all_to_all(parts, "y", 0, 0)
    shares = call(combine_body, [((H, DH, rows), bf16)], count=2, flops=2 * D * DH * rows)(parts, w_out)
    received = [passed_along(block, DOM, o) for block, o in zip(chosen, offsets(REACH))]
    shares = lax.all_to_all(shares, HEAD, 0, 0)
    base = call(
        message_body,
        [((DH, rows), f32)],
        scratch=[pltpu.VMEM((rows // bound + directions, D, bound), bf16)],
        smem=(6, 7),
        count=10,
        flops=2 * D * rows * (4 * bound + DH),
    )(x_full, *received, tile_vals, tile_counts, tile_cols, w_msg.T, x_own)
    return (base + shares.astype(f32).sum(axis=0)).astype(bf16).T


def solution(mesh):
    parts = Mesh(mesh.devices.reshape(PARTS), DOM + HEAD)
    placed = (
        P(DOM, HEAD),
        P(DOM, None, None, None),
        P(DOM),
        P(DOM, None),
        P(DOM, None, None),
        P(None, HEAD),
        P(None, None, HEAD),
        P(HEAD, None),
    )
    return jax.shard_map(local, mesh=parts, in_specs=placed, out_specs=P(DOM, HEAD), check_vma=False)
```

profile of v0, /device:TPU:6, one launch (start us, length us, event | category | flops | bytes accessed | tf_op | source)
XLA Modules:
  0.0 118.1 jit_solution(7542425644583147207)
XLA Ops:
  0.0 12.2 %all-gather = bf16[128,384]{1,0:T(8,128)(2,1)S(1)} all-gather(bf16[64,384]{1,0:T(8,128)(2,1)} %bitcast.11), channel_id=2, replica_groups=mesh['zl'=4,'y'=8,'c'=2,'zh'=2,'x'=4] {'zh'}, dimensions={0}, use_global_device_ids=true | all-gather | bytes 147456 | tf_op jit(solution)/shard_map/all_gather | solution.py:171
  12.3 0.0 copy-start.6
  12.3 10.3 %all_to_all.20.quad = bf16[4,2,64,384]{3,2,1,0:T(8,128)(2,1)S(1)} all-to-all(bf16[4,2,64,384]{3,2,1,0:T(8,128)(2,1)S(1)} %broadcast_in_dim.3), channel_id=1, replica_groups=mesh['zl'=4,'y'=8,'c'=2,'zh'=2,'x'=4] {'x'}, dimensions={0} | all-to-all | bytes 786432 | tf_op jit(solution)/shard_map/all_to_all | solution.py:39
  22.6 0.0 copy-start.7
  22.6 0.0 copy-done.6
  22.6 0.7 copy-done.7
  23.3 1.0 shard_map.82
  24.3 6.8 %all-to-all-start.1 = ((bf16[8,64,384]{2,1,0:T(8,128)(2,1)}), bf16[8,64,384]{2,1,0:T(8,128)(2,1)S(1)}, u32[]{:S(2)}, u32[]{:S(2)}) async-start(bf16[8,64,384]{2,1,0:T(8,128)(2,1)} %get-tuple-element.17), calls=%async_computation.1 | async-start | bytes 786432 | tf_op jit(solution)/shard_map/all_to_all | solution.py:181
  31.1 16.8 %all-gather.1 = bf16[1024,384]{1,0:T(8,128)(2,1)S(1)} all-gather(bf16[128,384]{1,0:T(8,128)(2,1)S(1)} %get-tuple-element.18), channel_id=3, replica_groups=mesh['zl'=4,'y'=8,'c'=2,'zh'=2,'x'=4] {'zl','c'}, dimensions={0}, use_global_device_ids=true | all-gather | bytes 884736 | tf_op jit(solution)/shard_map/all_gather | solution.py:182
  47.9 0.0 all-to-all-done.1.q
  47.9 14.2 %shard_map.84 = bf16[8,72,384]{2,1,0:T(8,128)(2,1)S(1)} custom-call(bf16[8,64,384]{2,1,0:T(8,128)(2,1)S(1)} %all-to-all-done.1.q, bf16[8,128,384]{2,1,0:T(8,128)(2,1)S(1)} %bitcast.10), custom_call_target="tpu_custom_call" | custom-call | flops 2415919104 | bytes 2000000 | tf_op jit(solution)/shard_map/pallas_call | solution.py:183
  62.1 0.0 copy-start.2
  62.1 23.4 %all_to_all.21.parts = bf16[8,72,384]{2,1,0:T(8,128)(2,1)S(1)} all-to-all(bf16[8,72,384]{2,1,0:T(8,128)(2,1)S(1)} %shard_map.84), channel_id=1, replica_groups=mesh['zl'=4,'y'=8,'c'=2,'zh'=2,'x'=4] {'y'}, dimensions={0} | all-to-all | bytes 884736 | tf_op jit(solution)/shard_map/all_to_all | solution.py:197
  85.6 0.0 copy-done.2
  85.6 1.1 shard_map.85
  86.7 0.0 copy-start
  86.7 0.0 copy-start.1
  86.7 0.0 copy-start.3
  86.7 9.2 %all-to-all-start.3 = ((bf16[8,64,384]{2,1,0:T(8,128)(2,1)}), bf16[8,64,384]{2,1,0:T(8,128)(2,1)S(1)}, u32[]{:S(2)}, u32[]{:S(2)}) async-start(bf16[8,64,384]{2,1,0:T(8,128)(2,1)} %shard_map.85), calls=%async_computation.3 | async-start | bytes 786432 | tf_op jit(solution)/shard_map/all_to_all | solution.py:200
  95.9 2.6 %collective-permute-start = (bf16[512,128]{1,0:T(8,128)(2,1)S(1)}, bf16[512,128]{1,0:T(8,128)(2,1)S(1)}, u32[]{:S(2)}, u32[]{:S(2)}) collective-permute-start(bf16[512,128]{1,0:T(8,128)(2,1)S(1)} %get-tuple-element.13), channel_id=1, source_target_pairs={{16,0},{24,8},{32,16},{40,24},{48,32},{56,40},{64,48},{72,56},{80,... | collective-permute-start | bytes 393224 | tf_op jit(solution)/shard_map/ppermute | solution.py:34
  98.5 2.3 %collective-permute-start.1 = (bf16[512,128]{1,0:T(8,128)(2,1)S(1)}, bf16[512,128]{1,0:T(8,128)(2,1)S(1)}, u32[]{:S(2)}, u32[]{:S(2)}) collective-permute-start(bf16[512,128]{1,0:T(8,128)(2,1)S(1)} %get-tuple-element.14), channel_id=1, source_target_pairs={{8,0},{16,8},{24,16},{32,24},{40,32},{48,40},{56,48},{64,56},{72,6... | collective-permute-start | bytes 393224 | tf_op jit(solution)/shard_map/ppermute | solution.py:34
  100.9 2.0 %collective-permute-start.2 = (bf16[512,128]{1,0:T(8,128)(2,1)S(1)}, bf16[512,128]{1,0:T(8,128)(2,1)S(1)}, u32[]{:S(2)}, u32[]{:S(2)}) collective-permute-start(bf16[512,128]{1,0:T(8,128)(2,1)S(1)} %get-tuple-element.15), channel_id=1, source_target_pairs={{504,0},{0,8},{8,16},{16,24},{24,32},{32,40},{40,48},{48,56},{56,6... | collective-permute-start | bytes 393224 | tf_op jit(solution)/shard_map/ppermute | solution.py:34
  102.9 0.0 copy-start.4
  102.9 3.2 %collective-permute-start.3 = (bf16[512,128]{1,0:T(8,128)(2,1)S(1)}, bf16[512,128]{1,0:T(8,128)(2,1)S(1)}, u32[]{:S(2)}, u32[]{:S(2)}) collective-permute-start(bf16[512,128]{1,0:T(8,128)(2,1)S(1)} %get-tuple-element.16), channel_id=1, source_target_pairs={{496,0},{504,8},{0,16},{8,24},{16,32},{24,40},{32,48},{40,56},{48,... | collective-permute-start | bytes 393224 | tf_op jit(solution)/shard_map/ppermute | solution.py:34
  106.1 0.0 collective-permute-done.r0
  106.1 0.0 collective-permute-done.1.r1
  106.1 5.0 %collective-permute-done.2.r2 = bf16[512,128]{1,0:T(8,128)(2,1)S(1)} collective-permute-done((bf16[512,128]{1,0:T(8,128)(2,1)S(1)}, bf16[512,128]{1,0:T(8,128)(2,1)S(1)}, u32[]{:S(2)}, u32[]{:S(2)}) %collective-permute-start.2) | collective-permute-done | bytes 131104 | tf_op jit(solution)/shard_map/ppermute | solution.py:34
  111.1 3.9 %collective-permute-done.3.r3 = bf16[512,128]{1,0:T(8,128)(2,1)S(1)} collective-permute-done((bf16[512,128]{1,0:T(8,128)(2,1)S(1)}, bf16[512,128]{1,0:T(8,128)(2,1)S(1)}, u32[]{:S(2)}, u32[]{:S(2)}) %collective-permute-start.3) | collective-permute-done | bytes 131104 | tf_op jit(solution)/shard_map/ppermute | solution.py:34
  115.0 0.0 copy-start.5
  115.0 0.0 copy-done
  115.0 0.0 copy-done.1
  115.0 0.0 copy-done.3
  115.0 0.0 copy-done.4
  115.0 0.6 copy-done.5
  115.6 1.8 %shard_map.83 = f32[64,384]{1,0:T(8,128)S(1)} custom-call(bf16[512,384]{1,0:T(8,128)(2,1)S(1)} %get-tuple-element.12.x, bf16[512,128]{1,0:T(8,128)(2,1)S(1)} %collective-permute-done.r0, bf16[512,128]{1,0:T(8,128)(2,1)S(1)} %collective-permute-done.1.r1, bf16[512,128]{1,0:T(8,128)(2,1)S(1)} %collective-permute-done.2.r2, ...), custom_call_target="tpu_custom_call" | custom-call | flops 226492416 | bytes 2000000 | tf_op jit(solution)/shard_map/pallas_call | solution.py:201
  117.4 0.0 all-to-all-done.3
  117.5 0.1 convert_reduce_fusion
  117.5 0.6 fusion
  (1 shorter events, 0.0 us)
Async XLA Ops:
  12.3 10.3 %copy-start.6 = (bf16[3,512,64]{1,2,0:T(8,128)(2,1)S(1)}, bf16[3,512,64]{1,2,0:T(8,128)(2,1)}, u32[]{:S(2)}) copy-start(bf16[3,512,64]{1,2,0:T(8,128)(2,1)} %param.14) | copy-start | bytes 589828
  22.6 0.7 copy-start.7
  24.3 23.7 %all-to-all-start.1 = ((bf16[8,64,384]{2,1,0:T(8,128)(2,1)}), bf16[8,64,384]{2,1,0:T(8,128)(2,1)S(1)}, u32[]{:S(2)}, u32[]{:S(2)}) async-start(bf16[8,64,384]{2,1,0:T(8,128)(2,1)} %get-tuple-element.17), calls=%async_computation.1 | async-start | bytes 786432 | tf_op jit(solution)/shard_map/all_to_all | solution.py:181
  62.1 23.5 %copy-start.2 = (bf16[64,512]{1,0:T(8,128)(2,1)S(1)}, bf16[64,512]{1,0:T(8,128)(2,1)}, u32[]{:S(2)}) copy-start(bf16[64,512]{1,0:T(8,128)(2,1)} %w_out.1) | copy-start | bytes 196612
  86.7 28.3 %copy-start = (bf16[3,4,128,128]{3,2,1,0:T(8,128)(2,1)S(1)}, bf16[3,4,128,128]{3,2,1,0:T(8,128)(2,1)}, u32[]{:S(2)}) copy-start(bf16[3,4,128,128]{3,2,1,0:T(8,128)(2,1)} %tiles.1) | copy-start | bytes 1179652
  86.7 28.3 %copy-start.1 = (bf16[384,64]{0,1:T(8,128)(2,1)S(1)}, bf16[384,64]{0,1:T(8,128)(2,1)}, u32[]{:S(2)}) copy-start(bf16[384,64]{0,1:T(8,128)(2,1)} %param.8) | copy-start | bytes 147460
  86.7 28.3 %copy-start.3 = (bf16[512,64]{0,1:T(8,128)(2,1)S(1)}, bf16[512,64]{0,1:T(8,128)(2,1)}, u32[]{:S(2)}) copy-start(bf16[512,64]{0,1:T(8,128)(2,1)} %param.13) | copy-start | bytes 196612
  86.7 30.7 %all-to-all-start.3 = ((bf16[8,64,384]{2,1,0:T(8,128)(2,1)}), bf16[8,64,384]{2,1,0:T(8,128)(2,1)S(1)}, u32[]{:S(2)}, u32[]{:S(2)}) async-start(bf16[8,64,384]{2,1,0:T(8,128)(2,1)} %shard_map.85), calls=%async_computation.3 | async-start | bytes 786432 | tf_op jit(solution)/shard_map/all_to_all | solution.py:200
  95.9 10.2 %collective-permute-start = (bf16[512,128]{1,0:T(8,128)(2,1)S(1)}, bf16[512,128]{1,0:T(8,128)(2,1)S(1)}, u32[]{:S(2)}, u32[]{:S(2)}) collective-permute-start(bf16[512,128]{1,0:T(8,128)(2,1)S(1)} %get-tuple-element.13), channel_id=1, source_target_pairs={{16,0},{24,8},{32,16},{40,24},{48,32},{56,40},{64,48},{72,56},{80,... | collective-permute-start | bytes 393224 | tf_op jit(solution)/shard_map/ppermute | solution.py:34
  98.5 7.6 %collective-permute-start.1 = (bf16[512,128]{1,0:T(8,128)(2,1)S(1)}, bf16[512,128]{1,0:T(8,128)(2,1)S(1)}, u32[]{:S(2)}, u32[]{:S(2)}) collective-permute-start(bf16[512,128]{1,0:T(8,128)(2,1)S(1)} %get-tuple-element.14), channel_id=1, source_target_pairs={{8,0},{16,8},{24,16},{32,24},{40,32},{48,40},{56,48},{64,56},{72,6... | collective-permute-start | bytes 393224 | tf_op jit(solution)/shard_map/ppermute | solution.py:34
  100.9 10.2 %collective-permute-start.2 = (bf16[512,128]{1,0:T(8,128)(2,1)S(1)}, bf16[512,128]{1,0:T(8,128)(2,1)S(1)}, u32[]{:S(2)}, u32[]{:S(2)}) collective-permute-start(bf16[512,128]{1,0:T(8,128)(2,1)S(1)} %get-tuple-element.15), channel_id=1, source_target_pairs={{504,0},{0,8},{8,16},{16,24},{24,32},{32,40},{40,48},{48,56},{56,6... | collective-permute-start | bytes 393224 | tf_op jit(solution)/shard_map/ppermute | solution.py:34
  102.9 12.1 %copy-start.4 = (s32[3,4]{1,0:T(4,128)S(1)}, s32[3,4]{1,0:T(4,128)}, u32[]{:S(2)}) copy-start(s32[3,4]{1,0:T(4,128)} %cols.1) | copy-start | bytes 148
  102.9 12.1 %collective-permute-start.3 = (bf16[512,128]{1,0:T(8,128)(2,1)S(1)}, bf16[512,128]{1,0:T(8,128)(2,1)S(1)}, u32[]{:S(2)}, u32[]{:S(2)}) collective-permute-start(bf16[512,128]{1,0:T(8,128)(2,1)S(1)} %get-tuple-element.16), channel_id=1, source_target_pairs={{496,0},{504,8},{0,16},{8,24},{16,32},{24,40},{32,48},{40,56},{48,... | collective-permute-start | bytes 393224 | tf_op jit(solution)/shard_map/ppermute | solution.py:34
  115.0 0.7 copy-start.5
where the time goes:
time: 119 us; the launch traced here: 118 us
  blocking collectives  62.8 us (53%)
  starting transfers between devices  26.2 us (22%)
  Pallas kernels  18.1 us (15%)
  waiting for transfers between devices  8.89 us (7%)
  local copies, waits for them, and re-layouts  1.38 us (1%)
    all_to_all x1, blocking collectives, local(): parts = lax.all_to_all(parts, 'y', 0, 0)  23.4 us
    all_gather x1, blocking collectives, local(): held = lax.all_gather(kv, ('zl', 'c'), axis=0, tiled=False)  16.8 us
    pallas_call x1, Pallas kernels, local(): call(attend_body, [((askers, CARRY, rows), bf16)], scratch=[pltpu.VMEM((k...  14.2 us
    all_gather x1, blocking collectives, local(): pair = lax.all_gather(x_own, 'zh', axis=0, tiled=False)  12.2 us
    all_to_all x1, blocking collectives, sent_to_all(): lax.all_to_all(jnp.broadcast_to(block, (size,) + block.shape), axis, 0, 0)  10.3 us
    ppermute x4, starting transfers between devices, passed_along(): lax.ppermute(block, axis, [((i - distance) % size, i) for i in range(size)])  10.2 us
    all_to_all x1, starting transfers between devices, local(): shares = lax.all_to_all(shares, HEAD, 0, 0)  9.17 us
    ppermute x4, waiting for transfers between devices, passed_along(): lax.ppermute(block, axis, [((i - distance) % size, i) for i in range(size)])  8.89 us
  transfers between devices with their start and end apart: 6, of which 2 were waited for; matrix products, arithmetic and copies ran while one was open for 0% of the time, Pallas kernels for 2%

commit v1 on v0

--- a/solution.py
+++ b/solution.py
@@ -17,8 +17,8 @@
 HEAD = ("zh", "x")
 PARTS = (4, 8, 2, 2, 4)
 CARRY = DH + 8
-TILE_Q = 1024
-TILE_K = 512
+TILE_Q = 256
+TILE_K = 256
 INTERPRET = False
 
 
@@ -62,7 +62,7 @@
     )
 
 
-def project_body(quad, weights, rows, q_out, kv_out, x_out, *chosen):
+def project_body(quad, weights, q_out, kv_out, x_out):
     per_z, per_x = quad.shape[1], quad.shape[0]
     for z in range(per_z):
         for x in range(per_x):
@@ -74,11 +74,13 @@
     for i in range(q_out.shape[0]):
         q_out[i] = query.astype(jnp.bfloat16)
     kv_out[...] = qkv[DH:].astype(jnp.bfloat16)
-    count = full.shape[1]
+
+
+def choose_body(x, rows, *chosen):
     for j, out in enumerate(chosen):
         listed = rows[j : j + 1, :]
-        spot = lax.broadcasted_iota(jnp.int32, (count, listed.shape[1]), 0) == listed
-        out[...] = matmul(full, spot.astype(jnp.bfloat16), ((1,), (0,))).astype(jnp.bfloat16)
+        spot = lax.broadcasted_iota(jnp.int32, (x.shape[1], listed.shape[1]), 0) == listed
+        out[...] = matmul(x[...], spot.astype(jnp.bfloat16), ((1,), (0,))).astype(jnp.bfloat16)
 
 
 def three(value):
@@ -88,37 +90,46 @@
     return [high, middle, rest - middle]
 
 
-def attend_body(q, kv, out, keys, values, queries, scores, weights, results):
+def attend_body(q, kv, out, keys, values, queries, scores_a, scores_b, weights_a, weights_b, results):
     blocks, _, width = kv.shape
     for j in range(blocks):
-        block = kv[j]
         at = slice(j * width, (j + 1) * width)
-        keys[at, :] = block[:DH].T
-        values[:DH, at] = block[DH:]
+        keys[at, :] = kv[j, :DH].T
+        values[:DH, at] = kv[j, DH:]
     values[DH:, :] = jnp.ones((CARRY - DH, blocks * width), jnp.bfloat16)
     count = q.shape[0]
     for i in range(count):
         queries[:, i * width : (i + 1) * width] = q[i]
     chunks = [slice(j * TILE_K, (j + 1) * TILE_K) for j in range(blocks * width // TILE_K)]
-
-    def step(tile, carried):
-        at = pl.multiple_of(tile * TILE_Q, TILE_Q)
-        asked = queries[:, pl.ds(at, TILE_Q)]
+    tiles = count * width // TILE_Q
+
+    def score(asked, scores, chunk, best):
+        part = matmul(keys[chunk, :], asked, ((1,), (0,)))
+        scores[chunk, :] = part
+        high = part.reshape(TILE_K // 8, 8, TILE_Q).max(axis=0)
+        return high if best is None else jnp.maximum(best, high)
+
+    def half(tile, scores, scores_next, weights, top):
+        following = pl.multiple_of(jnp.minimum(tile + 1, tiles - 1) * TILE_Q, TILE_Q)
+        asked = queries[:, pl.ds(following, TILE_Q)]
         best = None
         for chunk in chunks:
-            part = matmul(keys[chunk, :], asked, ((1,), (0,)))
-            scores[chunk, :] = part
-            high = part.reshape(TILE_K // 8, 8, TILE_Q).max(axis=0)
-            best = high if best is None else jnp.maximum(best, high)
-        top = best.max(axis=0, keepdims=True)
-        for chunk in chunks:
             weights[chunk, :] = jnp.exp(scores[chunk, :] - top).astype(jnp.bfloat16)
+            best = score(asked, scores_next, chunk, best)
         total = matmul(values[...], weights[...], ((1,), (0,)))
         rows = [total[:DH]] + three(top) + three(total[DH : DH + 1]) + [jnp.zeros((2, TILE_Q), jnp.float32)]
+        at = pl.multiple_of(tile * TILE_Q, TILE_Q)
         results[:, pl.ds(at, TILE_Q)] = jnp.concatenate(rows, axis=0).astype(jnp.bfloat16)
-        return carried
-
-    lax.fori_loop(0, count * width // TILE_Q, step, 0)
+        return best.max(axis=0, keepdims=True)
+
+    def step(pair, top):
+        top = half(2 * pair, scores_a, scores_b, weights_a, top)
+        return half(2 * pair + 1, scores_b, scores_a, weights_b, top)
+
+    best = None
+    for chunk in chunks:
+        best = score(queries[:, :TILE_Q], scores_a, chunk, best)
+    lax.fori_loop(0, tiles // 2, step, best.max(axis=0, keepdims=True))
     for i in range(count):
         out[i] = results[:, i * width : (i + 1) * width]
 
@@ -171,13 +182,12 @@
     pair = lax.all_gather(x_own, "zh", axis=0, tiled=False)
     quad = sent_to_all(pair, "x")
     weights = jnp.swapaxes(w_qkv, 1, 2).reshape(3 * DH, D)
-    q, kv, x_full, *chosen = call(
+    q, kv, x_full = call(
         project_body,
-        [((askers, DH, rows), bf16), ((2 * DH, rows), bf16), ((D, rows), bf16)]
-        + [((D, bound), bf16)] * directions,
-        count=3,
-        flops=2 * D * rows * (3 * DH + directions * bound),
-    )(quad, weights, listed)
+        [((askers, DH, rows), bf16), ((2 * DH, rows), bf16), ((D, rows), bf16)],
+        count=2,
+        flops=2 * D * rows * 3 * DH,
+    )(quad, weights)
     queries = lax.all_to_all(q, "y", 0, 0)
     held = lax.all_gather(kv, ("zl", "c"), axis=0, tiled=False)
     parts = call(
@@ -188,6 +198,8 @@
             pltpu.VMEM((CARRY, keys), bf16),
             pltpu.VMEM((DH, asked), bf16),
             pltpu.VMEM((keys, TILE_Q), f32),
+            pltpu.VMEM((keys, TILE_Q), f32),
+            pltpu.VMEM((keys, TILE_Q), bf16),
             pltpu.VMEM((keys, TILE_Q), bf16),
             pltpu.VMEM((CARRY, asked), bf16),
         ],
@@ -196,7 +208,15 @@
     )(queries, held)
     parts = lax.all_to_all(parts, "y", 0, 0)
     shares = call(combine_body, [((H, DH, rows), bf16)], count=2, flops=2 * D * DH * rows)(parts, w_out)
-    received = [passed_along(block, DOM, o) for block, o in zip(chosen, offsets(REACH))]
+    chosen = call(
+        choose_body,
+        [((D, bound), bf16)] * directions,
+        count=2,
+        flops=2 * D * rows * directions * bound,
+    )(x_full, listed)
+    received = []
+    for block, offset in zip(chosen, offsets(REACH)):
+        received.append(passed_along(block, DOM, offset))
     shares = lax.all_to_all(shares, HEAD, 0, 0)
     base = call(
         message_body,

time: 119 us -> 116 us (0.975)
  Pallas kernels: 18.1 us -> 16.5 us
  local copies, waits for them, and re-layouts: 1.38 us -> 0.08 us
    pallas_call x1, Pallas kernels: 14.2 us -> 12 us  [local(): call(attend_body, [((askers, CARRY, rows), bf16)], scratch=[pltpu.VMEM((k...]
    unnamed x16, local copies, waits for them, and re-layouts: 1.34 us -> 0.04 us
where the time goes in v1:
time: 116 us; the launch traced here: 115 us
  blocking collectives  62.8 us (54%)
  starting transfers between devices  26.2 us (23%)
  Pallas kernels  16.5 us (14%)
  waiting for transfers between devices  8.89 us (8%)
    all_to_all x1, blocking collectives, local(): parts = lax.all_to_all(parts, 'y', 0, 0)  23.5 us
    all_gather x1, blocking collectives, local(): held = lax.all_gather(kv, ('zl', 'c'), axis=0, tiled=False)  16.8 us
    all_gather x1, blocking collectives, local(): pair = lax.all_gather(x_own, 'zh', axis=0, tiled=False)  12.2 us
    pallas_call x1, Pallas kernels, local(): call(attend_body, [((askers, CARRY, rows), bf16)], scratch=[pltpu.VMEM((k...  12 us
    all_to_all x1, blocking collectives, sent_to_all(): lax.all_to_all(jnp.broadcast_to(block, (size,) + block.shape), axis, 0, 0)  10.3 us
    ppermute x4, starting transfers between devices, passed_along(): lax.ppermute(block, axis, [((i - distance) % size, i) for i in range(size)])  10.2 us
    all_to_all x1, starting transfers between devices, local(): shares = lax.all_to_all(shares, HEAD, 0, 0)  9.17 us
    ppermute x4, waiting for transfers between devices, passed_along(): lax.ppermute(block, axis, [((i - distance) % size, i) for i in range(size)])  8.89 us
  transfers between devices with their start and end apart: 6, of which 2 were waited for; matrix products, arithmetic and copies ran while one was open for 0% of the time, Pallas kernels for 2%

profile of v1, /device:TPU:6, one launch (start us, length us, event | category | flops | bytes accessed | tf_op | source)
XLA Modules:
  0.0 115.3 jit_solution(14265810088250965683)
XLA Ops:
  0.0 12.2 %all-gather = bf16[128,384]{1,0:T(8,128)(2,1)S(1)} all-gather(bf16[64,384]{1,0:T(8,128)(2,1)} %bitcast.11), channel_id=2, replica_groups=mesh['zl'=4,'y'=8,'c'=2,'zh'=2,'x'=4] {'zh'}, dimensions={0}, use_global_device_ids=true | all-gather | bytes 147456 | tf_op jit(solution)/shard_map/all_gather | solution.py:182
  12.3 0.0 copy-start.2
  12.3 10.3 %all_to_all.20.quad = bf16[4,2,64,384]{3,2,1,0:T(8,128)(2,1)S(1)} all-to-all(bf16[4,2,64,384]{3,2,1,0:T(8,128)(2,1)S(1)} %broadcast_in_dim.3), channel_id=1, replica_groups=mesh['zl'=4,'y'=8,'c'=2,'zh'=2,'x'=4] {'x'}, dimensions={0} | all-to-all | bytes 786432 | tf_op jit(solution)/shard_map/all_to_all | solution.py:39
  22.6 0.0 copy-done.2
  22.6 1.0 shard_map.82
  23.6 6.8 %all-to-all-start.1 = ((bf16[8,64,384]{2,1,0:T(8,128)(2,1)}), bf16[8,64,384]{2,1,0:T(8,128)(2,1)S(1)}, u32[]{:S(2)}, u32[]{:S(2)}) async-start(bf16[8,64,384]{2,1,0:T(8,128)(2,1)} %get-tuple-element.17), calls=%async_computation.1 | async-start | bytes 786432 | tf_op jit(solution)/shard_map/all_to_all | solution.py:191
  30.4 16.8 %all-gather.1 = bf16[1024,384]{1,0:T(8,128)(2,1)S(1)} all-gather(bf16[128,384]{1,0:T(8,128)(2,1)S(1)} %get-tuple-element.18), channel_id=3, replica_groups=mesh['zl'=4,'y'=8,'c'=2,'zh'=2,'x'=4] {'zl','c'}, dimensions={0}, use_global_device_ids=true | all-gather | bytes 884736 | tf_op jit(solution)/shard_map/all_gather | solution.py:192
  47.2 0.0 all-to-all-done.1.q
  47.2 12.0 %shard_map.85 = bf16[8,72,384]{2,1,0:T(8,128)(2,1)S(1)} custom-call(bf16[8,64,384]{2,1,0:T(8,128)(2,1)S(1)} %all-to-all-done.1.q, bf16[8,128,384]{2,1,0:T(8,128)(2,1)S(1)} %bitcast.10), custom_call_target="tpu_custom_call" | custom-call | flops 2415919104 | bytes 2000000 | tf_op jit(solution)/shard_map/pallas_call | solution.py:193
  59.3 0.0 copy-start.3
  59.3 23.5 %all_to_all.21.parts = bf16[8,72,384]{2,1,0:T(8,128)(2,1)S(1)} all-to-all(bf16[8,72,384]{2,1,0:T(8,128)(2,1)S(1)} %shard_map.85), channel_id=1, replica_groups=mesh['zl'=4,'y'=8,'c'=2,'zh'=2,'x'=4] {'y'}, dimensions={0} | all-to-all | bytes 884736 | tf_op jit(solution)/shard_map/all_to_all | solution.py:209
  82.7 0.0 copy-done.3
  82.7 1.1 shard_map.86
  83.9 0.0 copy-start.7
  83.9 9.2 %all-to-all-start.3 = ((bf16[8,64,384]{2,1,0:T(8,128)(2,1)}), bf16[8,64,384]{2,1,0:T(8,128)(2,1)S(1)}, u32[]{:S(2)}, u32[]{:S(2)}) async-start(bf16[8,64,384]{2,1,0:T(8,128)(2,1)} %shard_map.86), calls=%async_computation.3 | async-start | bytes 786432 | tf_op jit(solution)/shard_map/all_to_all | solution.py:220
  93.0 0.0 copy-start
  93.0 0.0 copy-done.7
  93.0 0.0 copy-start.1
  93.0 0.0 copy-start.4
  93.1 0.6 shard_map.83
  93.6 2.7 %collective-permute-start = (bf16[512,128]{1,0:T(8,128)(2,1)S(1)}, bf16[512,128]{1,0:T(8,128)(2,1)S(1)}, u32[]{:S(2)}, u32[]{:S(2)}) collective-permute-start(bf16[512,128]{1,0:T(8,128)(2,1)S(1)} %get-tuple-element.13), channel_id=1, source_target_pairs={{16,0},{24,8},{32,16},{40,24},{48,32},{56,40},{64,48},{72,56},{80,... | collective-permute-start | bytes 393224 | tf_op jit(solution)/shard_map/ppermute | solution.py:34
  96.3 2.3 %collective-permute-start.1 = (bf16[512,128]{1,0:T(8,128)(2,1)S(1)}, bf16[512,128]{1,0:T(8,128)(2,1)S(1)}, u32[]{:S(2)}, u32[]{:S(2)}) collective-permute-start(bf16[512,128]{1,0:T(8,128)(2,1)S(1)} %get-tuple-element.14), channel_id=1, source_target_pairs={{8,0},{16,8},{24,16},{32,24},{40,32},{48,40},{56,48},{64,56},{72,6... | collective-permute-start | bytes 393224 | tf_op jit(solution)/shard_map/ppermute | solution.py:34
  98.6 0.0 copy-start.5
  98.6 2.0 %collective-permute-start.2 = (bf16[512,128]{1,0:T(8,128)(2,1)S(1)}, bf16[512,128]{1,0:T(8,128)(2,1)S(1)}, u32[]{:S(2)}, u32[]{:S(2)}) collective-permute-start(bf16[512,128]{1,0:T(8,128)(2,1)S(1)} %get-tuple-element.15), channel_id=1, source_target_pairs={{504,0},{0,8},{8,16},{16,24},{24,32},{32,40},{40,48},{48,56},{56,6... | collective-permute-start | bytes 393224 | tf_op jit(solution)/shard_map/ppermute | solution.py:34
  100.6 0.0 copy-start.6
  100.7 3.2 %collective-permute-start.3 = (bf16[512,128]{1,0:T(8,128)(2,1)S(1)}, bf16[512,128]{1,0:T(8,128)(2,1)S(1)}, u32[]{:S(2)}, u32[]{:S(2)}) collective-permute-start(bf16[512,128]{1,0:T(8,128)(2,1)S(1)} %get-tuple-element.16), channel_id=1, source_target_pairs={{496,0},{504,8},{0,16},{8,24},{16,32},{24,40},{32,48},{40,56},{48,... | collective-permute-start | bytes 393224 | tf_op jit(solution)/shard_map/ppermute | solution.py:34
  103.9 0.0 collective-permute-done.r0
  103.9 0.0 collective-permute-done.1.r1
  103.9 4.9 %collective-permute-done.2.r2 = bf16[512,128]{1,0:T(8,128)(2,1)S(1)} collective-permute-done((bf16[512,128]{1,0:T(8,128)(2,1)S(1)}, bf16[512,128]{1,0:T(8,128)(2,1)S(1)}, u32[]{:S(2)}, u32[]{:S(2)}) %collective-permute-start.2) | collective-permute-done | bytes 131104 | tf_op jit(solution)/shard_map/ppermute | solution.py:34
  108.8 3.9 %collective-permute-done.3.r3 = bf16[512,128]{1,0:T(8,128)(2,1)S(1)} collective-permute-done((bf16[512,128]{1,0:T(8,128)(2,1)S(1)}, bf16[512,128]{1,0:T(8,128)(2,1)S(1)}, u32[]{:S(2)}, u32[]{:S(2)}) %collective-permute-start.3) | collective-permute-done | bytes 131104 | tf_op jit(solution)/shard_map/ppermute | solution.py:34
  112.8 0.0 copy-done
  112.8 0.0 copy-done.1
  112.8 0.0 copy-done.4
  112.8 0.0 copy-done.5
  112.8 0.0 copy-done.6
  112.8 1.8 %shard_map.84 = f32[64,384]{1,0:T(8,128)S(1)} custom-call(bf16[512,384]{1,0:T(8,128)(2,1)S(1)} %get-tuple-element.12.x, bf16[512,128]{1,0:T(8,128)(2,1)S(1)} %collective-permute-done.r0, bf16[512,128]{1,0:T(8,128)(2,1)S(1)} %collective-permute-done.1.r1, bf16[512,128]{1,0:T(8,128)(2,1)S(1)} %collective-permute-done.2.r2, ...), custom_call_target="tpu_custom_call" | custom-call | flops 226492416 | bytes 2000000 | tf_op jit(solution)/shard_map/pallas_call | solution.py:221
  114.6 0.0 all-to-all-done.3
  114.6 0.1 convert_reduce_fusion
  114.7 0.6 fusion
  (1 shorter events, 0.0 us)
Async XLA Ops:
  12.3 10.3 %copy-start.2 = (bf16[3,512,64]{1,2,0:T(8,128)(2,1)S(1)}, bf16[3,512,64]{1,2,0:T(8,128)(2,1)}, u32[]{:S(2)}) copy-start(bf16[3,512,64]{1,2,0:T(8,128)(2,1)} %param.14) | copy-start | bytes 589828
  23.6 23.7 %all-to-all-start.1 = ((bf16[8,64,384]{2,1,0:T(8,128)(2,1)}), bf16[8,64,384]{2,1,0:T(8,128)(2,1)S(1)}, u32[]{:S(2)}, u32[]{:S(2)}) async-start(bf16[8,64,384]{2,1,0:T(8,128)(2,1)} %get-tuple-element.17), calls=%async_computation.1 | async-start | bytes 786432 | tf_op jit(solution)/shard_map/all_to_all | solution.py:191
  59.3 23.5 %copy-start.3 = (bf16[64,512]{1,0:T(8,128)(2,1)S(1)}, bf16[64,512]{1,0:T(8,128)(2,1)}, u32[]{:S(2)}) copy-start(bf16[64,512]{1,0:T(8,128)(2,1)} %w_out.1) | copy-start | bytes 196612
  83.9 9.2 %copy-start.7 = (s32[1,4,128]{2,1,0:T(4,128)S(1)}, s32[1,4,128]{2,1,0:T(4,128)}, u32[]{:S(2)}) copy-start(s32[1,4,128]{2,1,0:T(4,128)} %param.12) | copy-start | bytes 6148
  83.9 30.7 %all-to-all-start.3 = ((bf16[8,64,384]{2,1,0:T(8,128)(2,1)}), bf16[8,64,384]{2,1,0:T(8,128)(2,1)S(1)}, u32[]{:S(2)}, u32[]{:S(2)}) async-start(bf16[8,64,384]{2,1,0:T(8,128)(2,1)} %shard_map.86), calls=%async_computation.3 | async-start | bytes 786432 | tf_op jit(solution)/shard_map/all_to_all | solution.py:220
  93.0 19.7 %copy-start = (bf16[3,4,128,128]{3,2,1,0:T(8,128)(2,1)S(1)}, bf16[3,4,128,128]{3,2,1,0:T(8,128)(2,1)}, u32[]{:S(2)}) copy-start(bf16[3,4,128,128]{3,2,1,0:T(8,128)(2,1)} %tiles.1) | copy-start | bytes 1179652
  93.0 19.7 %copy-start.1 = (bf16[384,64]{0,1:T(8,128)(2,1)S(1)}, bf16[384,64]{0,1:T(8,128)(2,1)}, u32[]{:S(2)}) copy-start(bf16[384,64]{0,1:T(8,128)(2,1)} %param.8) | copy-start | bytes 147460
  93.0 19.7 %copy-start.4 = (bf16[512,64]{0,1:T(8,128)(2,1)S(1)}, bf16[512,64]{0,1:T(8,128)(2,1)}, u32[]{:S(2)}) copy-start(bf16[512,64]{0,1:T(8,128)(2,1)} %param.13) | copy-start | bytes 196612
  93.6 10.2 %collective-permute-start = (bf16[512,128]{1,0:T(8,128)(2,1)S(1)}, bf16[512,128]{1,0:T(8,128)(2,1)S(1)}, u32[]{:S(2)}, u32[]{:S(2)}) collective-permute-start(bf16[512,128]{1,0:T(8,128)(2,1)S(1)} %get-tuple-element.13), channel_id=1, source_target_pairs={{16,0},{24,8},{32,16},{40,24},{48,32},{56,40},{64,48},{72,56},{80,... | collective-permute-start | bytes 393224 | tf_op jit(solution)/shard_map/ppermute | solution.py:34
  96.3 7.6 %collective-permute-start.1 = (bf16[512,128]{1,0:T(8,128)(2,1)S(1)}, bf16[512,128]{1,0:T(8,128)(2,1)S(1)}, u32[]{:S(2)}, u32[]{:S(2)}) collective-permute-start(bf16[512,128]{1,0:T(8,128)(2,1)S(1)} %get-tuple-element.14), channel_id=1, source_target_pairs={{8,0},{16,8},{24,16},{32,24},{40,32},{48,40},{56,48},{64,56},{72,6... | collective-permute-start | bytes 393224 | tf_op jit(solution)/shard_map/ppermute | solution.py:34
  98.6 14.2 %copy-start.5 = (s32[3,4]{1,0:T(4,128)S(1)}, s32[3,4]{1,0:T(4,128)}, u32[]{:S(2)}) copy-start(s32[3,4]{1,0:T(4,128)} %cols.1) | copy-start | bytes 148
  98.6 10.2 %collective-permute-start.2 = (bf16[512,128]{1,0:T(8,128)(2,1)S(1)}, bf16[512,128]{1,0:T(8,128)(2,1)S(1)}, u32[]{:S(2)}, u32[]{:S(2)}) collective-permute-start(bf16[512,128]{1,0:T(8,128)(2,1)S(1)} %get-tuple-element.15), channel_id=1, source_target_pairs={{504,0},{0,8},{8,16},{16,24},{24,32},{32,40},{40,48},{48,56},{56,6... | collective-permute-start | bytes 393224 | tf_op jit(solution)/shard_map/ppermute | solution.py:34
  100.6 12.1 %copy-start.6 = (s32[3]{0:T(128)S(1)}, s32[3]{0:T(128)}, u32[]{:S(2)}) copy-start(s32[3]{0:T(128)} %counts.1) | copy-start | bytes 40
  100.7 12.1 %collective-permute-start.3 = (bf16[512,128]{1,0:T(8,128)(2,1)S(1)}, bf16[512,128]{1,0:T(8,128)(2,1)S(1)}, u32[]{:S(2)}, u32[]{:S(2)}) collective-permute-start(bf16[512,128]{1,0:T(8,128)(2,1)S(1)} %get-tuple-element.16), channel_id=1, source_target_pairs={{496,0},{504,8},{0,16},{8,24},{16,32},{24,40},{32,48},{40,56},{48,... | collective-permute-start | bytes 393224 | tf_op jit(solution)/shard_map/ppermute | solution.py:34

commit v2 on v1

--- a/solution.py
+++ b/solution.py
@@ -22,13 +22,6 @@
 INTERPRET = False
 
 
-def offsets(reach_count):
-    return [
-        position - reach_count if position < reach_count else position - reach_count + 1
-        for position in range(2 * reach_count)
-    ]
-
-
 def passed_along(block, axis, distance):
     size = lax.axis_size(axis)
     return lax.ppermute(block, axis, [((i - distance) % size, i) for i in range(size)])
@@ -43,9 +36,10 @@
     return lax.dot_general(a, b, ((contract[0], contract[1]), ((), ())), preferred_element_type=jnp.float32)
 
 
-def call(body, outs, scratch=(), smem=(), count=0, flops=0):
+def call(body, outs, scratch=(), smem=(), hbm=(), count=0, flops=0):
     specs = [
-        pl.BlockSpec(memory_space=pltpu.SMEM if i in smem else pltpu.VMEM) for i in range(count)
+        pl.BlockSpec(memory_space=pltpu.SMEM if i in smem else pltpu.HBM if i in hbm else pltpu.VMEM)
+        for i in range(count)
     ]
     outputs = [jax.ShapeDtypeStruct(shape, dtype) for shape, dtype in outs]
     return pl.pallas_call(
@@ -76,13 +70,6 @@
     kv_out[...] = qkv[DH:].astype(jnp.bfloat16)
 
 
-def choose_body(x, rows, *chosen):
-    for j, out in enumerate(chosen):
-        listed = rows[j : j + 1, :]
-        spot = lax.broadcasted_iota(jnp.int32, (x.shape[1], listed.shape[1]), 0) == listed
-        out[...] = matmul(x[...], spot.astype(jnp.bfloat16), ((1,), (0,))).astype(jnp.bfloat16)
-
-
 def three(value):
     high = value.astype(jnp.bfloat16).astype(jnp.float32)
     rest = value - high
@@ -90,7 +77,9 @@
     return [high, middle, rest - middle]
 
 
-def attend_body(q, kv, out, keys, values, queries, scores_a, scores_b, weights_a, weights_b, results):
+def attend_body(q, kv, x, rows, out, down, up, partner, cross, keys, values, queries, scores_a, scores_b, weights_a, weights_b, results, lists, arrived):
+    fetch = pltpu.make_async_copy(rows, lists, arrived)
+    fetch.start()
     blocks, _, width = kv.shape
     for j in range(blocks):
         at = slice(j * width, (j + 1) * width)
@@ -132,6 +121,12 @@
     lax.fori_loop(0, tiles // 2, step, best.max(axis=0, keepdims=True))
     for i in range(count):
         out[i] = results[:, i * width : (i + 1) * width]
+    fetch.wait()
+    core = lax.axis_index("c")
+    for j, chosen in ((0, down), (2 * REACH - 1, up), (REACH - core, partner), (REACH - 1 + core, cross)):
+        listed = lists[pl.ds(j, 1), :]
+        spot = lax.broadcasted_iota(jnp.int32, (x.shape[1], listed.shape[1]), 0) == listed
+        chosen[...] = matmul(x[...], spot.astype(jnp.bfloat16), ((1,), (0,))).astype(jnp.bfloat16)
 
 
 def combine_body(parts, w_out, out):
@@ -154,11 +149,12 @@
         out[h] = share.astype(jnp.bfloat16)
 
 
-def message_body(x, r0, r1, r2, r3, tiles, counts, cols, w_msg, own_x, out, table):
+def message_body(x, down, up, partner, cross, tiles, counts, cols, w_msg, own_x, out, table):
     own, slots, size, _ = tiles.shape
     for b in range(own):
         table[b] = x[:, b * size : (b + 1) * size]
-    for j, received in enumerate((r0, r1, r2, r3)):
+    core = lax.axis_index("c")
+    for j, received in ((0, down), (2 * REACH - 1, up), (REACH - 1 + core, partner), (REACH - core, cross)):
         table[own + j] = received[...]
     for r in range(own):
         total = jnp.zeros((D, size), jnp.float32)
@@ -190,9 +186,9 @@
     )(quad, weights)
     queries = lax.all_to_all(q, "y", 0, 0)
     held = lax.all_gather(kv, ("zl", "c"), axis=0, tiled=False)
-    parts = call(
+    parts, down, up, partner, cross = call(
         attend_body,
-        [((askers, CARRY, rows), bf16)],
+        [((askers, CARRY, rows), bf16)] + [((D, bound), bf16)] * directions,
         scratch=[
             pltpu.VMEM((keys, DH), bf16),
             pltpu.VMEM((CARRY, keys), bf16),
@@ -202,21 +198,20 @@
             pltpu.VMEM((keys, TILE_Q), bf16),
             pltpu.VMEM((keys, TILE_Q), bf16),
             pltpu.VMEM((CARRY, asked), bf16),
+            pltpu.VMEM((directions, bound), jnp.int32),
+            pltpu.SemaphoreType.DMA,
         ],
-        count=2,
+        hbm=(3,),
+        count=4,
         flops=4 * DH * keys * asked,
-    )(queries, held)
+    )(queries, held, x_full, listed)
     parts = lax.all_to_all(parts, "y", 0, 0)
     shares = call(combine_body, [((H, DH, rows), bf16)], count=2, flops=2 * D * DH * rows)(parts, w_out)
-    chosen = call(
-        choose_body,
-        [((D, bound), bf16)] * directions,
-        count=2,
-        flops=2 * D * rows * directions * bound,
-    )(x_full, listed)
-    received = []
-    for block, offset in zip(chosen, offsets(REACH)):
-        received.append(passed_along(block, DOM, offset))
+    down = passed_along(down, DOM, -REACH)
+    up = passed_along(up, DOM, REACH)
+    size = lax.axis_size(DOM)
+    cross = lax.ppermute(cross, DOM, [(i, (i + (1 if i % 2 else -1)) % size) for i in range(size)])
+    partner = passed_along(partner, "c", 1)
     shares = lax.all_to_all(shares, HEAD, 0, 0)
     base = call(
         message_body,
@@ -225,7 +220,7 @@
         smem=(6, 7),
         count=10,
         flops=2 * D * rows * (4 * bound + DH),
-    )(x_full, *received, tile_vals, tile_counts, tile_cols, w_msg.T, x_own)
+    )(x_full, down, up, partner, cross, tile_vals, tile_counts, tile_cols, w_msg.T, x_own)
     return (base + shares.astype(f32).sum(axis=0)).astype(bf16).T
 
 

time: 116 us -> 115 us (level)
  waiting for transfers between devices: 8.89 us -> 3.4 us
  starting transfers between devices: 26.2 us -> 30.5 us
    ppermute x4 -> x3, waiting for transfers between devices: 8.89 us -> 0.01 us  [passed_along(): lax.ppermute(block, axis, [((i - distance) % size, i) for i in range(size)])]
    ppermute x0 -> x1, starting transfers between devices: none -> 6.77 us  [local(): lax.ppermute(cross, DOM, [(i, (i + (1 if i % 2 else -1)) % size) for i in...]
    ppermute x0 -> x1, waiting for transfers between devices: none -> 3.38 us  [local(): lax.ppermute(cross, DOM, [(i, (i + (1 if i % 2 else -1)) % size) for i in...]
    ppermute x4 -> x3, starting transfers between devices: 10.2 us -> 7.75 us  [passed_along(): lax.ppermute(block, axis, [((i - distance) % size, i) for i in range(size)])]
    pallas_call x2 -> x1, Pallas kernels: 12.6 us -> 12.7 us  [local(): call(attend_body, [((askers, CARRY, rows), bf16)] + [((D, bound), bf16)]...]
  transfers between devices with their start and end apart: 6 -> 6, of which waited for: 2 -> 1; matrix products, arithmetic and copies ran while one was open for 0% -> 0% of each run, Pallas kernels for 2% -> 2%
where the time goes in v2:
time: 115 us
  blocking collectives  62.8 us (55%)
  starting transfers between devices  30.5 us (27%)
  Pallas kernels  16.6 us (14%)
  waiting for transfers between devices  3.4 us (3%)
    all_to_all x1, blocking collectives, local(): parts = lax.all_to_all(parts, 'y', 0, 0)  23.4 us
    all_gather x1, blocking collectives, local(): held = lax.all_gather(kv, ('zl', 'c'), axis=0, tiled=False)  16.8 us
    pallas_call x1, Pallas kernels, local(): call(attend_body, [((askers, CARRY, rows), bf16)] + [((D, bound), bf16)]...  12.7 us
    all_gather x1, blocking collectives, local(): pair = lax.all_gather(x_own, 'zh', axis=0, tiled=False)  12.2 us
    all_to_all x1, blocking collectives, sent_to_all(): lax.all_to_all(jnp.broadcast_to(block, (size,) + block.shape), axis, 0, 0)  10.3 us
    all_to_all x1, starting transfers between devices, local(): shares = lax.all_to_all(shares, HEAD, 0, 0)  9.14 us
    ppermute x3, starting transfers between devices, passed_along(): lax.ppermute(block, axis, [((i - distance) % size, i) for i in range(size)])  7.75 us
    all_to_all x1, starting transfers between devices, local(): queries = lax.all_to_all(q, 'y', 0, 0)  6.83 us
  transfers between devices with their start and end apart: 6, of which 1 were waited for; matrix products, arithmetic and copies ran while one was open for 0% of the time, Pallas kernels for 2%

profile of v2, /device:TPU:6, one launch (start us, length us, event | category | flops | bytes accessed | tf_op | source)
XLA Modules:
  0.0 114.8 jit_solution(11020759146567408433)
XLA Ops:
  0.0 12.2 %all-gather = bf16[128,384]{1,0:T(8,128)(2,1)S(1)} all-gather(bf16[64,384]{1,0:T(8,128)(2,1)} %bitcast.11), channel_id=2, replica_groups=mesh['zl'=4,'y'=8,'c'=2,'zh'=2,'x'=4] {'zh'}, dimensions={0}, use_global_device_ids=true | all-gather | bytes 147456 | tf_op jit(solution)/shard_map/all_gather | solution.py:178
  12.3 0.0 copy-start.2
  12.3 10.3 %all_to_all.20.quad = bf16[4,2,64,384]{3,2,1,0:T(8,128)(2,1)S(1)} all-to-all(bf16[4,2,64,384]{3,2,1,0:T(8,128)(2,1)S(1)} %broadcast_in_dim.3), channel_id=1, replica_groups=mesh['zl'=4,'y'=8,'c'=2,'zh'=2,'x'=4] {'x'}, dimensions={0} | all-to-all | bytes 786432 | tf_op jit(solution)/shard_map/all_to_all | solution.py:32
  22.6 0.0 copy-done.2
  22.6 1.0 shard_map.82
  23.6 6.8 %all-to-all-start.1 = ((bf16[8,64,384]{2,1,0:T(8,128)(2,1)}), bf16[8,64,384]{2,1,0:T(8,128)(2,1)S(1)}, u32[]{:S(2)}, u32[]{:S(2)}) async-start(bf16[8,64,384]{2,1,0:T(8,128)(2,1)} %get-tuple-element.14), calls=%async_computation.1 | async-start | bytes 786432 | tf_op jit(solution)/shard_map/all_to_all | solution.py:187
  30.4 16.8 %all-gather.1 = bf16[1024,384]{1,0:T(8,128)(2,1)S(1)} all-gather(bf16[128,384]{1,0:T(8,128)(2,1)S(1)} %get-tuple-element.15), channel_id=3, replica_groups=mesh['zl'=4,'y'=8,'c'=2,'zh'=2,'x'=4] {'zl','c'}, dimensions={0}, use_global_device_ids=true | all-gather | bytes 884736 | tf_op jit(solution)/shard_map/all_gather | solution.py:188
  47.2 0.0 all-to-all-done.1.q
  47.2 0.0 copy-start.7
  47.2 0.7 copy-done.7
  47.9 12.7 %shard_map.83 = (bf16[8,72,384]{2,1,0:T(8,128)(2,1)S(1)}, bf16[512,128]{1,0:T(8,128)(2,1)S(1)}, bf16[512,128]{1,0:T(8,128)(2,1)S(1)}, bf16[512,128]{1,0:T(8,128)(2,1)S(1)}, bf16[512,128]{1,0:T(8,128)(2,1)S(1)}) custom-call(bf16[8,64,384]{2,1,0:T(8,128)(2,1)S(1)} %all-to-all-done.1.q, bf16[8,128,384]{2,1,0:T(8,128)(2,1)S(1)} %bitcast.10, ...), custom_call_target="tpu_custom_call" | custom-call | flops 2415919104 | bytes 2000000 | tf_op jit(solution)/shard_map/pallas_call | solution.py:189
  60.6 0.0 copy-start.3
  60.6 23.4 %all_to_all.21.parts = bf16[8,72,384]{2,1,0:T(8,128)(2,1)S(1)} all-to-all(bf16[8,72,384]{2,1,0:T(8,128)(2,1)S(1)} %get-tuple-element.20), channel_id=1, replica_groups=mesh['zl'=4,'y'=8,'c'=2,'zh'=2,'x'=4] {'y'}, dimensions={0} | all-to-all | bytes 884736 | tf_op jit(solution)/shard_map/all_to_all | solution.py:208
  84.0 0.0 copy-done.3
  84.0 1.1 shard_map.85
  85.2 0.0 copy-start
  85.2 0.0 copy-start.1
  85.2 0.0 copy-start.4
  85.2 9.1 %all-to-all-start.3 = ((bf16[8,64,384]{2,1,0:T(8,128)(2,1)}), bf16[8,64,384]{2,1,0:T(8,128)(2,1)S(1)}, u32[]{:S(2)}, u32[]{:S(2)}) async-start(bf16[8,64,384]{2,1,0:T(8,128)(2,1)} %shard_map.85), calls=%async_computation.3 | async-start | bytes 786432 | tf_op jit(solution)/shard_map/all_to_all | solution.py:215
  94.3 2.8 %collective-permute-start = (bf16[512,128]{1,0:T(8,128)(2,1)S(1)}, bf16[512,128]{1,0:T(8,128)(2,1)S(1)}, u32[]{:S(2)}, u32[]{:S(2)}) collective-permute-start(bf16[512,128]{1,0:T(8,128)(2,1)S(1)} %get-tuple-element.16), channel_id=1, source_target_pairs={{16,0},{24,8},{32,16},{40,24},{48,32},{56,40},{64,48},{72,56},{80,... | collective-permute-start | bytes 393224 | tf_op jit(solution)/shard_map/ppermute | solution.py:27
  97.1 3.1 %collective-permute-start.1 = (bf16[512,128]{1,0:T(8,128)(2,1)S(1)}, bf16[512,128]{1,0:T(8,128)(2,1)S(1)}, u32[]{:S(2)}, u32[]{:S(2)}) collective-permute-start(bf16[512,128]{1,0:T(8,128)(2,1)S(1)} %get-tuple-element.17), channel_id=1, source_target_pairs={{496,0},{504,8},{0,16},{8,24},{16,32},{24,40},{32,48},{40,56},{48,... | collective-permute-start | bytes 393224 | tf_op jit(solution)/shard_map/ppermute | solution.py:27
  100.1 0.0 copy-start.5
  100.2 1.9 %collective-permute-start.2 = (bf16[512,128]{1,0:T(8,128)(2,1)S(1)}, bf16[512,128]{1,0:T(8,128)(2,1)S(1)}, u32[]{:S(2)}, u32[]{:S(2)}) collective-permute-start(bf16[512,128]{1,0:T(8,128)(2,1)S(1)} %get-tuple-element.18), channel_id=1, source_target_pairs={{8,0},{0,8},{9,1},{1,9},{10,2},{2,10},{11,3},{3,11},{12,4},{4,12},... | collective-permute-start | bytes 393224 | tf_op jit(solution)/shard_map/ppermute | solution.py:27
  102.1 0.0 copy-start.6
  102.1 6.8 %collective-permute-start.3 = (bf16[512,128]{1,0:T(8,128)(2,1)S(1)}, bf16[512,128]{1,0:T(8,128)(2,1)S(1)}, u32[]{:S(2)}, u32[]{:S(2)}) collective-permute-start(bf16[512,128]{1,0:T(8,128)(2,1)S(1)} %get-tuple-element.19), channel_id=1, source_target_pairs={{0,504},{8,16},{16,8},{24,32},{32,24},{40,48},{48,40},{56,64},{64,... | collective-permute-start | bytes 393224 | tf_op jit(solution)/shard_map/ppermute | solution.py:213
  108.9 0.0 collective-permute-done.down
  108.9 0.0 collective-permute-done.1.up
  108.9 0.0 collective-permute-done.2.partner
  108.9 3.4 %collective-permute-done.3.cross = bf16[512,128]{1,0:T(8,128)(2,1)S(1)} collective-permute-done((bf16[512,128]{1,0:T(8,128)(2,1)S(1)}, bf16[512,128]{1,0:T(8,128)(2,1)S(1)}, u32[]{:S(2)}, u32[]{:S(2)}) %collective-permute-start.3) | collective-permute-done | bytes 131104 | tf_op jit(solution)/shard_map/ppermute | solution.py:213
  112.3 0.0 copy-done
  112.3 0.0 copy-done.1
  112.3 0.0 copy-done.4
  112.3 0.0 copy-done.5
  112.3 0.0 copy-done.6
  112.3 1.8 %shard_map.84 = f32[64,384]{1,0:T(8,128)S(1)} custom-call(bf16[512,384]{1,0:T(8,128)(2,1)S(1)} %get-tuple-element.13.x, bf16[512,128]{1,0:T(8,128)(2,1)S(1)} %collective-permute-done.down, bf16[512,128]{1,0:T(8,128)(2,1)S(1)} %collective-permute-done.1.up, bf16[512,128]{1,0:T(8,128)(2,1)S(1)} %collective-permute-done.2.partner, ...), custom_call_target="tpu_custom_call" | custom-call | flops 226492416 | bytes 2000000 | tf_op jit(solution)/shard_map/pallas_call | solution.py:216
  114.1 0.0 all-to-all-done.3
  114.1 0.1 convert_reduce_fusion
  114.2 0.6 fusion
  (1 shorter events, 0.0 us)
Async XLA Ops:
  12.3 10.3 %copy-start.2 = (bf16[3,512,64]{1,2,0:T(8,128)(2,1)S(1)}, bf16[3,512,64]{1,2,0:T(8,128)(2,1)}, u32[]{:S(2)}) copy-start(bf16[3,512,64]{1,2,0:T(8,128)(2,1)} %param.14) | copy-start | bytes 589828
  23.6 23.7 %all-to-all-start.1 = ((bf16[8,64,384]{2,1,0:T(8,128)(2,1)}), bf16[8,64,384]{2,1,0:T(8,128)(2,1)S(1)}, u32[]{:S(2)}, u32[]{:S(2)}) async-start(bf16[8,64,384]{2,1,0:T(8,128)(2,1)} %get-tuple-element.14), calls=%async_computation.1 | async-start | bytes 786432 | tf_op jit(solution)/shard_map/all_to_all | solution.py:187
  47.2 0.7 copy-start.7
  60.6 23.4 %copy-start.3 = (bf16[64,512]{1,0:T(8,128)(2,1)S(1)}, bf16[64,512]{1,0:T(8,128)(2,1)}, u32[]{:S(2)}) copy-start(bf16[64,512]{1,0:T(8,128)(2,1)} %w_out.1) | copy-start | bytes 196612
  85.2 27.1 %copy-start = (bf16[3,4,128,128]{3,2,1,0:T(8,128)(2,1)S(1)}, bf16[3,4,128,128]{3,2,1,0:T(8,128)(2,1)}, u32[]{:S(2)}) copy-start(bf16[3,4,128,128]{3,2,1,0:T(8,128)(2,1)} %tiles.1) | copy-start | bytes 1179652
  85.2 27.1 %copy-start.1 = (bf16[384,64]{0,1:T(8,128)(2,1)S(1)}, bf16[384,64]{0,1:T(8,128)(2,1)}, u32[]{:S(2)}) copy-start(bf16[384,64]{0,1:T(8,128)(2,1)} %param.8) | copy-start | bytes 147460
  85.2 27.1 %copy-start.4 = (bf16[512,64]{0,1:T(8,128)(2,1)S(1)}, bf16[512,64]{0,1:T(8,128)(2,1)}, u32[]{:S(2)}) copy-start(bf16[512,64]{0,1:T(8,128)(2,1)} %param.13) | copy-start | bytes 196612
  85.2 29.0 %all-to-all-start.3 = ((bf16[8,64,384]{2,1,0:T(8,128)(2,1)}), bf16[8,64,384]{2,1,0:T(8,128)(2,1)S(1)}, u32[]{:S(2)}, u32[]{:S(2)}) async-start(bf16[8,64,384]{2,1,0:T(8,128)(2,1)} %shard_map.85), calls=%async_computation.3 | async-start | bytes 786432 | tf_op jit(solution)/shard_map/all_to_all | solution.py:215
  94.3 14.6 %collective-permute-start = (bf16[512,128]{1,0:T(8,128)(2,1)S(1)}, bf16[512,128]{1,0:T(8,128)(2,1)S(1)}, u32[]{:S(2)}, u32[]{:S(2)}) collective-permute-start(bf16[512,128]{1,0:T(8,128)(2,1)S(1)} %get-tuple-element.16), channel_id=1, source_target_pairs={{16,0},{24,8},{32,16},{40,24},{48,32},{56,40},{64,48},{72,56},{80,... | collective-permute-start | bytes 393224 | tf_op jit(solution)/shard_map/ppermute | solution.py:27
  97.1 11.8 %collective-permute-start.1 = (bf16[512,128]{1,0:T(8,128)(2,1)S(1)}, bf16[512,128]{1,0:T(8,128)(2,1)S(1)}, u32[]{:S(2)}, u32[]{:S(2)}) collective-permute-start(bf16[512,128]{1,0:T(8,128)(2,1)S(1)} %get-tuple-element.17), channel_id=1, source_target_pairs={{496,0},{504,8},{0,16},{8,24},{16,32},{24,40},{32,48},{40,56},{48,... | collective-permute-start | bytes 393224 | tf_op jit(solution)/shard_map/ppermute | solution.py:27
  100.1 12.2 %copy-start.5 = (s32[3,4]{1,0:T(4,128)S(1)}, s32[3,4]{1,0:T(4,128)}, u32[]{:S(2)}) copy-start(s32[3,4]{1,0:T(4,128)} %cols.1) | copy-start | bytes 148
  100.2 8.7 %collective-permute-start.2 = (bf16[512,128]{1,0:T(8,128)(2,1)S(1)}, bf16[512,128]{1,0:T(8,128)(2,1)S(1)}, u32[]{:S(2)}, u32[]{:S(2)}) collective-permute-start(bf16[512,128]{1,0:T(8,128)(2,1)S(1)} %get-tuple-element.18), channel_id=1, source_target_pairs={{8,0},{0,8},{9,1},{1,9},{10,2},{2,10},{11,3},{3,11},{12,4},{4,12},... | collective-permute-start | bytes 393224 | tf_op jit(solution)/shard_map/ppermute | solution.py:27
  102.1 10.2 %copy-start.6 = (s32[3]{0:T(128)S(1)}, s32[3]{0:T(128)}, u32[]{:S(2)}) copy-start(s32[3]{0:T(128)} %counts.1) | copy-start | bytes 40
  102.1 10.2 %collective-permute-start.3 = (bf16[512,128]{1,0:T(8,128)(2,1)S(1)}, bf16[512,128]{1,0:T(8,128)(2,1)S(1)}, u32[]{:S(2)}, u32[]{:S(2)}) collective-permute-start(bf16[512,128]{1,0:T(8,128)(2,1)S(1)} %get-tuple-element.19), channel_id=1, source_target_pairs={{0,504},{8,16},{16,8},{24,32},{32,24},{40,48},{48,40},{56,64},{64,... | collective-permute-start | bytes 393224 | tf_op jit(solution)/shard_map/ppermute | solution.py:213

commit v3 on v2

--- a/solution.py
+++ b/solution.py
@@ -144,9 +144,20 @@
         total = total + factor * sums[i]
         value = value + factor * parts[i, :DH, :].astype(jnp.float32)
     heads_out = (value / total).astype(jnp.bfloat16)
-    for h in range(H):
-        share = matmul(w_out[:, h * DH : (h + 1) * DH], heads_out, ((0,), (0,)))
-        out[h] = share.astype(jnp.bfloat16)
+    per_x, per_z = out.shape[:2]
+    for z in range(per_z):
+        for x in range(per_x):
+            at = (z * per_x + x) * DH
+            share = matmul(w_out[:, at : at + DH], heads_out, ((0,), (0,)))
+            out[x, z] = share.astype(jnp.bfloat16)
+
+
+def fold_body(shares, keep, send):
+    mine = lax.axis_index("zh")
+    total = [shares[x, mine].astype(jnp.float32) for x in range(shares.shape[0])]
+    keep[...] = sum(total[1:], total[0])
+    total = [shares[x, 1 - mine].astype(jnp.float32) for x in range(shares.shape[0])]
+    send[...] = sum(total[1:], total[0]).astype(jnp.bfloat16)
 
 
 def message_body(x, down, up, partner, cross, tiles, counts, cols, w_msg, own_x, out, table):
@@ -204,15 +215,18 @@
         hbm=(3,),
         count=4,
         flops=4 * DH * keys * asked,
-    )(queries, held, x_full, listed)
+    )(queries, held, x_full, pltpu.with_memory_space_constraint(listed, pltpu.HBM))
     parts = lax.all_to_all(parts, "y", 0, 0)
-    shares = call(combine_body, [((H, DH, rows), bf16)], count=2, flops=2 * D * DH * rows)(parts, w_out)
+    per_x, per_z = lax.axis_size("x"), lax.axis_size("zh")
+    shares = call(
+        combine_body, [((per_x, per_z, DH, rows), bf16)], count=2, flops=2 * D * DH * rows
+    )(parts, w_out)
     down = passed_along(down, DOM, -REACH)
     up = passed_along(up, DOM, REACH)
     size = lax.axis_size(DOM)
     cross = lax.ppermute(cross, DOM, [(i, (i + (1 if i % 2 else -1)) % size) for i in range(size)])
     partner = passed_along(partner, "c", 1)
-    shares = lax.all_to_all(shares, HEAD, 0, 0)
+    shares = lax.all_to_all(shares, "x", 0, 0)
     base = call(
         message_body,
         [((DH, rows), f32)],
@@ -221,7 +235,12 @@
         count=10,
         flops=2 * D * rows * (4 * bound + DH),
     )(x_full, down, up, partner, cross, tile_vals, tile_counts, tile_cols, w_msg.T, x_own)
-    return (base + shares.astype(f32).sum(axis=0)).astype(bf16).T
+    keep, send = call(
+        fold_body, [((DH, rows), f32), ((DH, rows), bf16)], count=1, flops=D * rows
+    )(shares)
+    halves = lax.all_gather(send, "zh", axis=0, tiled=False)
+    others = jnp.where(lax.axis_index("zh") == 0, halves[1], halves[0])
+    return (base + keep + others.astype(f32)).astype(bf16).T
 
 
 def solution(mesh):

time: 115 us -> 120 us (1.043)
  blocking collectives: 62.8 us -> 71.4 us
  starting transfers between devices: 30.5 us -> 26.1 us
    all_gather x0 -> x1, blocking collectives: none -> 8.67 us  [local(): halves = lax.all_gather(send, 'zh', axis=0, tiled=False)]
    all_to_all x1, starting transfers between devices: 9.14 us -> 5.63 us  [local(): shares = lax.all_to_all(shares, 'x', 0, 0)]
where the time goes in v3:
time: 120 us; the launch traced here: 119 us
  blocking collectives  71.4 us (60%)
  starting transfers between devices  26.1 us (22%)
  Pallas kernels  16.7 us (14%)
  waiting for transfers between devices  4.21 us (4%)
    all_to_all x1, blocking collectives, local(): parts = lax.all_to_all(parts, 'y', 0, 0)  23.4 us
    all_gather x1, blocking collectives, local(): held = lax.all_gather(kv, ('zl', 'c'), axis=0, tiled=False)  16.8 us
    pallas_call x1, Pallas kernels, local(): call(attend_body, [((askers, CARRY, rows), bf16)] + [((D, bound), bf16)]...  12.7 us
    all_gather x1, blocking collectives, local(): pair = lax.all_gather(x_own, 'zh', axis=0, tiled=False)  12.2 us
    all_to_all x1, blocking collectives, sent_to_all(): lax.all_to_all(jnp.broadcast_to(block, (size,) + block.shape), axis, 0, 0)  10.3 us
    all_gather x1, blocking collectives, local(): halves = lax.all_gather(send, 'zh', axis=0, tiled=False)  8.67 us
    ppermute x3, starting transfers between devices, passed_along(): lax.ppermute(block, axis, [((i - distance) % size, i) for i in range(size)])  7.75 us
    all_to_all x1, starting transfers between devices, local(): queries = lax.all_to_all(q, 'y', 0, 0)  6.83 us
  transfers between devices with their start and end apart: 6, of which 1 were waited for; matrix products, arithmetic and copies ran while one was open for 0% of the time, Pallas kernels for 2%

profile of v3, /device:TPU:6, one launch (start us, length us, event | category | flops | bytes accessed | tf_op | source)
XLA Modules:
  0.0 119.3 jit_solution(2509406469069578618)
XLA Ops:
  0.0 12.2 %all-gather = bf16[128,384]{1,0:T(8,128)(2,1)S(1)} all-gather(bf16[64,384]{1,0:T(8,128)(2,1)} %bitcast.11), channel_id=2, replica_groups=mesh['zl'=4,'y'=8,'c'=2,'zh'=2,'x'=4] {'zh'}, dimensions={0}, use_global_device_ids=true | all-gather | bytes 147456 | tf_op jit(solution)/shard_map/all_gather | solution.py:189
  12.3 0.0 copy-start.2
  12.3 10.3 %all_to_all.20.quad = bf16[4,2,64,384]{3,2,1,0:T(8,128)(2,1)S(1)} all-to-all(bf16[4,2,64,384]{3,2,1,0:T(8,128)(2,1)S(1)} %broadcast_in_dim.3), channel_id=1, replica_groups=mesh['zl'=4,'y'=8,'c'=2,'zh'=2,'x'=4] {'x'}, dimensions={0} | all-to-all | bytes 786432 | tf_op jit(solution)/shard_map/all_to_all | solution.py:32
  22.6 0.0 copy-done.2
  22.6 1.0 shard_map.82
  23.6 6.8 %all-to-all-start.1 = ((bf16[8,64,384]{2,1,0:T(8,128)(2,1)}), bf16[8,64,384]{2,1,0:T(8,128)(2,1)S(1)}, u32[]{:S(2)}, u32[]{:S(2)}) async-start(bf16[8,64,384]{2,1,0:T(8,128)(2,1)} %get-tuple-element.16), calls=%async_computation.1 | async-start | bytes 786432 | tf_op jit(solution)/shard_map/all_to_all | solution.py:198
  30.4 16.8 %all-gather.1 = bf16[1024,384]{1,0:T(8,128)(2,1)S(1)} all-gather(bf16[128,384]{1,0:T(8,128)(2,1)S(1)} %get-tuple-element.17), channel_id=3, replica_groups=mesh['zl'=4,'y'=8,'c'=2,'zh'=2,'x'=4] {'zl','c'}, dimensions={0}, use_global_device_ids=true | all-gather | bytes 884736 | tf_op jit(solution)/shard_map/all_gather | solution.py:199
  47.2 0.0 all-to-all-done.1.q
  47.2 12.7 %shard_map.83 = (bf16[8,72,384]{2,1,0:T(8,128)(2,1)S(1)}, bf16[512,128]{1,0:T(8,128)(2,1)S(1)}, bf16[512,128]{1,0:T(8,128)(2,1)S(1)}, bf16[512,128]{1,0:T(8,128)(2,1)S(1)}, bf16[512,128]{1,0:T(8,128)(2,1)S(1)}) custom-call(bf16[8,64,384]{2,1,0:T(8,128)(2,1)S(1)} %all-to-all-done.1.q, bf16[8,128,384]{2,1,0:T(8,128)(2,1)S(1)} %bitcast.10, ...), custom_call_target="tpu_custom_call" | custom-call | flops 2415919104 | bytes 2000000 | tf_op jit(solution)/shard_map/pallas_call | solution.py:200
  59.9 0.0 copy-start.3
  59.9 23.4 %all_to_all.21.parts = bf16[8,72,384]{2,1,0:T(8,128)(2,1)S(1)} all-to-all(bf16[8,72,384]{2,1,0:T(8,128)(2,1)S(1)} %get-tuple-element.22), channel_id=1, replica_groups=mesh['zl'=4,'y'=8,'c'=2,'zh'=2,'x'=4] {'y'}, dimensions={0} | all-to-all | bytes 884736 | tf_op jit(solution)/shard_map/all_to_all | solution.py:219
  83.4 0.0 copy-done.3
  83.4 1.1 shard_map.85
  84.5 0.0 copy-start
  84.5 0.0 copy-start.1
  84.5 0.0 copy-start.4
  84.5 5.6 %all-to-all-start.3 = ((bf16[4,2,64,384]{3,2,1,0:T(8,128)(2,1)}), bf16[4,2,64,384]{3,2,1,0:T(8,128)(2,1)S(1)}, u32[]{:S(2)}, u32[]{:S(2)}) async-start(bf16[4,2,64,384]{3,2,1,0:T(8,128)(2,1)} %shard_map.85), calls=%async_computation.3 | async-start | bytes 786432 | tf_op jit(solution)/shard_map/all_to_all | solution.py:229
  90.1 1.9 %collective-permute-start = (bf16[512,128]{1,0:T(8,128)(2,1)S(1)}, bf16[512,128]{1,0:T(8,128)(2,1)S(1)}, u32[]{:S(2)}, u32[]{:S(2)}) collective-permute-start(bf16[512,128]{1,0:T(8,128)(2,1)S(1)} %get-tuple-element.18), channel_id=1, source_target_pairs={{16,0},{24,8},{32,16},{40,24},{48,32},{56,40},{64,48},{72,56},{80,... | collective-permute-start | bytes 393224 | tf_op jit(solution)/shard_map/ppermute | solution.py:27
  92.1 3.9 %collective-permute-start.1 = (bf16[512,128]{1,0:T(8,128)(2,1)S(1)}, bf16[512,128]{1,0:T(8,128)(2,1)S(1)}, u32[]{:S(2)}, u32[]{:S(2)}) collective-permute-start(bf16[512,128]{1,0:T(8,128)(2,1)S(1)} %get-tuple-element.19), channel_id=1, source_target_pairs={{496,0},{504,8},{0,16},{8,24},{16,32},{24,40},{32,48},{40,56},{48,... | collective-permute-start | bytes 393224 | tf_op jit(solution)/shard_map/ppermute | solution.py:27
  96.0 1.9 %collective-permute-start.2 = (bf16[512,128]{1,0:T(8,128)(2,1)S(1)}, bf16[512,128]{1,0:T(8,128)(2,1)S(1)}, u32[]{:S(2)}, u32[]{:S(2)}) collective-permute-start(bf16[512,128]{1,0:T(8,128)(2,1)S(1)} %get-tuple-element.20), channel_id=1, source_target_pairs={{8,0},{0,8},{9,1},{1,9},{10,2},{2,10},{11,3},{3,11},{12,4},{4,12},... | collective-permute-start | bytes 393224 | tf_op jit(solution)/shard_map/ppermute | solution.py:27
  97.9 5.9 %collective-permute-start.3 = (bf16[512,128]{1,0:T(8,128)(2,1)S(1)}, bf16[512,128]{1,0:T(8,128)(2,1)S(1)}, u32[]{:S(2)}, u32[]{:S(2)}) collective-permute-start(bf16[512,128]{1,0:T(8,128)(2,1)S(1)} %get-tuple-element.21), channel_id=1, source_target_pairs={{0,504},{8,16},{16,8},{24,32},{32,24},{40,48},{48,40},{56,64},{64,... | collective-permute-start | bytes 393224 | tf_op jit(solution)/shard_map/ppermute | solution.py:227
  103.9 0.0 copy-start.5
  103.9 0.0 copy-start.6
  103.9 0.0 collective-permute-done.down
  103.9 0.0 collective-permute-done.1.up
  103.9 0.0 collective-permute-done.2.partner
  103.9 4.2 %collective-permute-done.3.cross = bf16[512,128]{1,0:T(8,128)(2,1)S(1)} collective-permute-done((bf16[512,128]{1,0:T(8,128)(2,1)S(1)}, bf16[512,128]{1,0:T(8,128)(2,1)S(1)}, u32[]{:S(2)}, u32[]{:S(2)}) %collective-permute-start.3) | collective-permute-done | bytes 131104 | tf_op jit(solution)/shard_map/ppermute | solution.py:227
  108.1 0.0 copy-done
  108.1 0.0 copy-done.1
  108.1 0.0 copy-done.4
  108.1 0.0 copy-done.5
  108.1 0.0 copy-done.6
  108.1 1.8 %shard_map.84 = f32[64,384]{1,0:T(8,128)S(1)} custom-call(bf16[512,384]{1,0:T(8,128)(2,1)S(1)} %get-tuple-element.15.x, bf16[512,128]{1,0:T(8,128)(2,1)S(1)} %collective-permute-done.down, bf16[512,128]{1,0:T(8,128)(2,1)S(1)} %collective-permute-done.1.up, bf16[512,128]{1,0:T(8,128)(2,1)S(1)} %collective-permute-done.2.partner, ...), custom_call_target="tpu_custom_call" | custom-call | flops 226492416 | bytes 2000000 | tf_op jit(solution)/shard_map/pallas_call | solution.py:230
  110.0 0.0 all-to-all-done.3.shares
  110.0 0.1 shard_map.86
  110.0 8.7 %all-gather.2 = bf16[128,384]{1,0:T(8,128)(2,1)S(1)} all-gather(bf16[64,384]{1,0:T(8,128)(2,1)S(1)} %get-tuple-element.24), channel_id=4, replica_groups=mesh['zl'=4,'y'=8,'c'=2,'zh'=2,'x'=4] {'zh'}, dimensions={0}, use_global_device_ids=true | all-gather | bytes 147456 | tf_op jit(solution)/shard_map/all_gather | solution.py:241
  118.7 0.6 fusion.1
  (1 shorter events, 0.0 us)
Async XLA Ops:
  12.3 10.3 %copy-start.2 = (bf16[3,512,64]{1,2,0:T(8,128)(2,1)S(1)}, bf16[3,512,64]{1,2,0:T(8,128)(2,1)}, u32[]{:S(2)}) copy-start(bf16[3,512,64]{1,2,0:T(8,128)(2,1)} %param.14) | copy-start | bytes 589828
  23.6 23.7 %all-to-all-start.1 = ((bf16[8,64,384]{2,1,0:T(8,128)(2,1)}), bf16[8,64,384]{2,1,0:T(8,128)(2,1)S(1)}, u32[]{:S(2)}, u32[]{:S(2)}) async-start(bf16[8,64,384]{2,1,0:T(8,128)(2,1)} %get-tuple-element.16), calls=%async_computation.1 | async-start | bytes 786432 | tf_op jit(solution)/shard_map/all_to_all | solution.py:198
  59.9 23.5 %copy-start.3 = (bf16[64,512]{1,0:T(8,128)(2,1)S(1)}, bf16[64,512]{1,0:T(8,128)(2,1)}, u32[]{:S(2)}) copy-start(bf16[64,512]{1,0:T(8,128)(2,1)} %w_out.1) | copy-start | bytes 196612
  84.5 23.6 %copy-start = (bf16[3,4,128,128]{3,2,1,0:T(8,128)(2,1)S(1)}, bf16[3,4,128,128]{3,2,1,0:T(8,128)(2,1)}, u32[]{:S(2)}) copy-start(bf16[3,4,128,128]{3,2,1,0:T(8,128)(2,1)} %tiles.1) | copy-start | bytes 1179652
  84.5 23.6 %copy-start.1 = (bf16[384,64]{0,1:T(8,128)(2,1)S(1)}, bf16[384,64]{0,1:T(8,128)(2,1)}, u32[]{:S(2)}) copy-start(bf16[384,64]{0,1:T(8,128)(2,1)} %param.8) | copy-start | bytes 147460
  84.5 23.6 %copy-start.4 = (bf16[512,64]{0,1:T(8,128)(2,1)S(1)}, bf16[512,64]{0,1:T(8,128)(2,1)}, u32[]{:S(2)}) copy-start(bf16[512,64]{0,1:T(8,128)(2,1)} %param.13) | copy-start | bytes 196612
  84.5 25.4 %all-to-all-start.3 = ((bf16[4,2,64,384]{3,2,1,0:T(8,128)(2,1)}), bf16[4,2,64,384]{3,2,1,0:T(8,128)(2,1)S(1)}, u32[]{:S(2)}, u32[]{:S(2)}) async-start(bf16[4,2,64,384]{3,2,1,0:T(8,128)(2,1)} %shard_map.85), calls=%async_computation.3 | async-start | bytes 786432 | tf_op jit(solution)/shard_map/all_to_all | solution.py:229
  90.1 13.7 %collective-permute-start = (bf16[512,128]{1,0:T(8,128)(2,1)S(1)}, bf16[512,128]{1,0:T(8,128)(2,1)S(1)}, u32[]{:S(2)}, u32[]{:S(2)}) collective-permute-start(bf16[512,128]{1,0:T(8,128)(2,1)S(1)} %get-tuple-element.18), channel_id=1, source_target_pairs={{16,0},{24,8},{32,16},{40,24},{48,32},{56,40},{64,48},{72,56},{80,... | collective-permute-start | bytes 393224 | tf_op jit(solution)/shard_map/ppermute | solution.py:27
  92.1 11.8 %collective-permute-start.1 = (bf16[512,128]{1,0:T(8,128)(2,1)S(1)}, bf16[512,128]{1,0:T(8,128)(2,1)S(1)}, u32[]{:S(2)}, u32[]{:S(2)}) collective-permute-start(bf16[512,128]{1,0:T(8,128)(2,1)S(1)} %get-tuple-element.19), channel_id=1, source_target_pairs={{496,0},{504,8},{0,16},{8,24},{16,32},{24,40},{32,48},{40,56},{48,... | collective-permute-start | bytes 393224 | tf_op jit(solution)/shard_map/ppermute | solution.py:27
  96.0 7.9 %collective-permute-start.2 = (bf16[512,128]{1,0:T(8,128)(2,1)S(1)}, bf16[512,128]{1,0:T(8,128)(2,1)S(1)}, u32[]{:S(2)}, u32[]{:S(2)}) collective-permute-start(bf16[512,128]{1,0:T(8,128)(2,1)S(1)} %get-tuple-element.20), channel_id=1, source_target_pairs={{8,0},{0,8},{9,1},{1,9},{10,2},{2,10},{11,3},{3,11},{12,4},{4,12},... | collective-permute-start | bytes 393224 | tf_op jit(solution)/shard_map/ppermute | solution.py:27
  97.9 10.2 %collective-permute-start.3 = (bf16[512,128]{1,0:T(8,128)(2,1)S(1)}, bf16[512,128]{1,0:T(8,128)(2,1)S(1)}, u32[]{:S(2)}, u32[]{:S(2)}) collective-permute-start(bf16[512,128]{1,0:T(8,128)(2,1)S(1)} %get-tuple-element.21), channel_id=1, source_target_pairs={{0,504},{8,16},{16,8},{24,32},{32,24},{40,48},{48,40},{56,64},{64,... | collective-permute-start | bytes 393224 | tf_op jit(solution)/shard_map/ppermute | solution.py:227
  103.9 4.3 %copy-start.5 = (s32[3,4]{1,0:T(4,128)S(1)}, s32[3,4]{1,0:T(4,128)}, u32[]{:S(2)}) copy-start(s32[3,4]{1,0:T(4,128)} %cols.1) | copy-start | bytes 148
  103.9 4.3 %copy-start.6 = (s32[3]{0:T(128)S(1)}, s32[3]{0:T(128)}, u32[]{:S(2)}) copy-start(s32[3]{0:T(128)} %counts.1) | copy-start | bytes 40

commit v4 on v3

--- a/solution.py
+++ b/solution.py
@@ -20,6 +20,13 @@
 TILE_Q = 256
 TILE_K = 256
 INTERPRET = False
+
+
+def offsets(reach_count):
+    return [
+        position - reach_count if position < reach_count else position - reach_count + 1
+        for position in range(2 * reach_count)
+    ]
 
 
 def passed_along(block, axis, distance):
@@ -77,7 +84,8 @@
     return [high, middle, rest - middle]
 
 
-def attend_body(q, kv, x, rows, out, down, up, partner, cross, keys, values, queries, scores_a, scores_b, weights_a, weights_b, results, lists, arrived):
+def attend_body(q, kv, x, rows, out, *rest):
+    *chosen, keys, values, queries, scores_a, scores_b, weights_a, weights_b, results, lists, arrived = rest
     fetch = pltpu.make_async_copy(rows, lists, arrived)
     fetch.start()
     blocks, _, width = kv.shape
@@ -122,11 +130,10 @@
     for i in range(count):
         out[i] = results[:, i * width : (i + 1) * width]
     fetch.wait()
-    core = lax.axis_index("c")
-    for j, chosen in ((0, down), (2 * REACH - 1, up), (REACH - core, partner), (REACH - 1 + core, cross)):
-        listed = lists[pl.ds(j, 1), :]
+    for j, block in enumerate(chosen):
+        listed = lists[j : j + 1, :]
         spot = lax.broadcasted_iota(jnp.int32, (x.shape[1], listed.shape[1]), 0) == listed
-        chosen[...] = matmul(x[...], spot.astype(jnp.bfloat16), ((1,), (0,))).astype(jnp.bfloat16)
+        block[...] = matmul(x[...], spot.astype(jnp.bfloat16), ((1,), (0,))).astype(jnp.bfloat16)
 
 
 def combine_body(parts, w_out, out):
@@ -160,12 +167,11 @@
     send[...] = sum(total[1:], total[0]).astype(jnp.bfloat16)
 
 
-def message_body(x, down, up, partner, cross, tiles, counts, cols, w_msg, own_x, out, table):
+def message_body(x, r0, r1, r2, r3, tiles, counts, cols, w_msg, own_x, out, table):
     own, slots, size, _ = tiles.shape
     for b in range(own):
         table[b] = x[:, b * size : (b + 1) * size]
-    core = lax.axis_index("c")
-    for j, received in ((0, down), (2 * REACH - 1, up), (REACH - 1 + core, partner), (REACH - core, cross)):
+    for j, received in enumerate((r0, r1, r2, r3)):
         table[own + j] = received[...]
     for r in range(own):
         total = jnp.zeros((D, size), jnp.float32)
@@ -197,7 +203,7 @@
     )(quad, weights)
     queries = lax.all_to_all(q, "y", 0, 0)
     held = lax.all_gather(kv, ("zl", "c"), axis=0, tiled=False)
-    parts, down, up, partner, cross = call(
+    parts, *chosen = call(
         attend_body,
         [((askers, CARRY, rows), bf16)] + [((D, bound), bf16)] * directions,
         scratch=[
@@ -221,11 +227,9 @@
     shares = call(
         combine_body, [((per_x, per_z, DH, rows), bf16)], count=2, flops=2 * D * DH * rows
     )(parts, w_out)
-    down = passed_along(down, DOM, -REACH)
-    up = passed_along(up, DOM, REACH)
-    size = lax.axis_size(DOM)
-    cross = lax.ppermute(cross, DOM, [(i, (i + (1 if i % 2 else -1)) % size) for i in range(size)])
-    partner = passed_along(partner, "c", 1)
+    received = []
+    for block, offset in zip(chosen, offsets(REACH)):
+        received.append(passed_along(block, DOM, offset))
     shares = lax.all_to_all(shares, "x", 0, 0)
     base = call(
         message_body,
@@ -234,7 +238,7 @@
         smem=(6, 7),
         count=10,
         flops=2 * D * rows * (4 * bound + DH),
-    )(x_full, down, up, partner, cross, tile_vals, tile_counts, tile_cols, w_msg.T, x_own)
+    )(x_full, *received, tile_vals, tile_counts, tile_cols, w_msg.T, x_own)
     keep, send = call(
         fold_body, [((DH, rows), f32), ((DH, rows), bf16)], count=1, flops=D * rows
     )(shares)

time: 120 us -> 121 us (level)
  waiting for transfers between devices: 4.21 us -> 7.75 us
  starting transfers between devices: 26.1 us -> 22.6 us
  blocking collectives: 71.4 us -> 72.8 us
    ppermute x3 -> x4, waiting for transfers between devices: 0.01 us -> 7.74 us  [passed_along(): lax.ppermute(block, axis, [((i - distance) % size, i) for i in range(size)])]
    ppermute x1 -> x0, starting transfers between devices: 5.93 us -> none  [local(): lax.ppermute(cross, DOM, [(i, (i + (1 if i % 2 else -1)) % size) for i in...]
    ppermute x1 -> x0, waiting for transfers between devices: 4.19 us -> none  [local(): lax.ppermute(cross, DOM, [(i, (i + (1 if i % 2 else -1)) % size) for i in...]
    ppermute x3 -> x4, starting transfers between devices: 7.75 us -> 10.2 us  [passed_along(): lax.ppermute(block, axis, [((i - distance) % size, i) for i in range(size)])]
    all_gather x1, blocking collectives: 8.67 us -> 9.97 us  [local(): halves = lax.all_gather(send, 'zh', axis=0, tiled=False)]
  transfers between devices with their start and end apart: 6 -> 6, of which waited for: 1 -> 2; matrix products, arithmetic and copies ran while one was open for 0% -> 0% of each run, Pallas kernels for 2% -> 1%
where the time goes in v4:
time: 121 us
  blocking collectives  72.8 us (60%)
  starting transfers between devices  22.6 us (19%)
  Pallas kernels  16.7 us (14%)
  waiting for transfers between devices  7.75 us (6%)
    all_to_all x1, blocking collectives, local(): parts = lax.all_to_all(parts, 'y', 0, 0)  23.5 us
    all_gather x1, blocking collectives, local(): held = lax.all_gather(kv, ('zl', 'c'), axis=0, tiled=False)  16.8 us
    pallas_call x1, Pallas kernels, local(): call(attend_body, [((askers, CARRY, rows), bf16)] + [((D, bound), bf16)]...  12.7 us
    all_gather x1, blocking collectives, local(): pair = lax.all_gather(x_own, 'zh', axis=0, tiled=False)  12.2 us
    all_to_all x1, blocking collectives, sent_to_all(): lax.all_to_all(jnp.broadcast_to(block, (size,) + block.shape), axis, 0, 0)  10.3 us
    ppermute x4, starting transfers between devices, passed_along(): lax.ppermute(block, axis, [((i - distance) % size, i) for i in range(size)])  10.2 us
    all_gather x1, blocking collectives, local(): halves = lax.all_gather(send, 'zh', axis=0, tiled=False)  9.97 us
    ppermute x4, waiting for transfers between devices, passed_along(): lax.ppermute(block, axis, [((i - distance) % size, i) for i in range(size)])  7.74 us
  transfers between devices with their start and end apart: 6, of which 2 were waited for; matrix products, arithmetic and copies ran while one was open for 0% of the time, Pallas kernels for 1%

profile of v4, /device:TPU:6, one launch (start us, length us, event | category | flops | bytes accessed | tf_op | source)
XLA Modules:
  0.0 120.7 jit_solution(9815908088904244088)
XLA Ops:
  0.0 12.2 %all-gather = bf16[128,384]{1,0:T(8,128)(2,1)S(1)} all-gather(bf16[64,384]{1,0:T(8,128)(2,1)} %bitcast.11), channel_id=2, replica_groups=mesh['zl'=4,'y'=8,'c'=2,'zh'=2,'x'=4] {'zh'}, dimensions={0}, use_global_device_ids=true | all-gather | bytes 147456 | tf_op jit(solution)/shard_map/all_gather | solution.py:195
  12.3 0.0 copy-start.2
  12.3 10.3 %all_to_all.20.quad = bf16[4,2,64,384]{3,2,1,0:T(8,128)(2,1)S(1)} all-to-all(bf16[4,2,64,384]{3,2,1,0:T(8,128)(2,1)S(1)} %broadcast_in_dim.3), channel_id=1, replica_groups=mesh['zl'=4,'y'=8,'c'=2,'zh'=2,'x'=4] {'x'}, dimensions={0} | all-to-all | bytes 786432 | tf_op jit(solution)/shard_map/all_to_all | solution.py:39
  22.6 0.0 copy-done.2
  22.6 1.0 shard_map.82
  23.6 6.8 %all-to-all-start.1 = ((bf16[8,64,384]{2,1,0:T(8,128)(2,1)}), bf16[8,64,384]{2,1,0:T(8,128)(2,1)S(1)}, u32[]{:S(2)}, u32[]{:S(2)}) async-start(bf16[8,64,384]{2,1,0:T(8,128)(2,1)} %get-tuple-element.16), calls=%async_computation.1 | async-start | bytes 786432 | tf_op jit(solution)/shard_map/all_to_all | solution.py:204
  30.4 16.8 %all-gather.1 = bf16[1024,384]{1,0:T(8,128)(2,1)S(1)} all-gather(bf16[128,384]{1,0:T(8,128)(2,1)S(1)} %get-tuple-element.17), channel_id=3, replica_groups=mesh['zl'=4,'y'=8,'c'=2,'zh'=2,'x'=4] {'zl','c'}, dimensions={0}, use_global_device_ids=true | all-gather | bytes 884736 | tf_op jit(solution)/shard_map/all_gather | solution.py:205
  47.2 0.0 all-to-all-done.1.q
  47.2 12.7 %shard_map.83 = (bf16[8,72,384]{2,1,0:T(8,128)(2,1)S(1)}, bf16[512,128]{1,0:T(8,128)(2,1)S(1)}, bf16[512,128]{1,0:T(8,128)(2,1)S(1)}, bf16[512,128]{1,0:T(8,128)(2,1)S(1)}, bf16[512,128]{1,0:T(8,128)(2,1)S(1)}) custom-call(bf16[8,64,384]{2,1,0:T(8,128)(2,1)S(1)} %all-to-all-done.1.q, bf16[8,128,384]{2,1,0:T(8,128)(2,1)S(1)} %bitcast.10, ...), custom_call_target="tpu_custom_call" | custom-call | flops 2415919104 | bytes 2000000 | tf_op jit(solution)/shard_map/pallas_call | solution.py:206
  59.9 0.0 copy-start.3
  59.9 23.5 %all_to_all.21.parts = bf16[8,72,384]{2,1,0:T(8,128)(2,1)S(1)} all-to-all(bf16[8,72,384]{2,1,0:T(8,128)(2,1)S(1)} %get-tuple-element.22), channel_id=1, replica_groups=mesh['zl'=4,'y'=8,'c'=2,'zh'=2,'x'=4] {'y'}, dimensions={0} | all-to-all | bytes 884736 | tf_op jit(solution)/shard_map/all_to_all | solution.py:225
  83.4 0.0 copy-done.3
  83.4 1.1 shard_map.85
  84.5 0.0 copy-start
  84.5 0.0 copy-start.1
  84.5 0.0 copy-start.4
  84.5 5.6 %all-to-all-start.3 = ((bf16[4,2,64,384]{3,2,1,0:T(8,128)(2,1)}), bf16[4,2,64,384]{3,2,1,0:T(8,128)(2,1)S(1)}, u32[]{:S(2)}, u32[]{:S(2)}) async-start(bf16[4,2,64,384]{3,2,1,0:T(8,128)(2,1)} %shard_map.85), calls=%async_computation.3 | async-start | bytes 786432 | tf_op jit(solution)/shard_map/all_to_all | solution.py:233
  90.2 1.9 %collective-permute-start = (bf16[512,128]{1,0:T(8,128)(2,1)S(1)}, bf16[512,128]{1,0:T(8,128)(2,1)S(1)}, u32[]{:S(2)}, u32[]{:S(2)}) collective-permute-start(bf16[512,128]{1,0:T(8,128)(2,1)S(1)} %get-tuple-element.18), channel_id=1, source_target_pairs={{16,0},{24,8},{32,16},{40,24},{48,32},{56,40},{64,48},{72,56},{80,... | collective-permute-start | bytes 393224 | tf_op jit(solution)/shard_map/ppermute | solution.py:34
  92.1 2.5 %collective-permute-start.1 = (bf16[512,128]{1,0:T(8,128)(2,1)S(1)}, bf16[512,128]{1,0:T(8,128)(2,1)S(1)}, u32[]{:S(2)}, u32[]{:S(2)}) collective-permute-start(bf16[512,128]{1,0:T(8,128)(2,1)S(1)} %get-tuple-element.19), channel_id=1, source_target_pairs={{8,0},{16,8},{24,16},{32,24},{40,32},{48,40},{56,48},{64,56},{72,6... | collective-permute-start | bytes 393224 | tf_op jit(solution)/shard_map/ppermute | solution.py:34
  94.6 1.9 %collective-permute-start.2 = (bf16[512,128]{1,0:T(8,128)(2,1)S(1)}, bf16[512,128]{1,0:T(8,128)(2,1)S(1)}, u32[]{:S(2)}, u32[]{:S(2)}) collective-permute-start(bf16[512,128]{1,0:T(8,128)(2,1)S(1)} %get-tuple-element.20), channel_id=1, source_target_pairs={{504,0},{0,8},{8,16},{16,24},{24,32},{32,40},{40,48},{48,56},{56,6... | collective-permute-start | bytes 393224 | tf_op jit(solution)/shard_map/ppermute | solution.py:34
  96.5 3.8 %collective-permute-start.3 = (bf16[512,128]{1,0:T(8,128)(2,1)S(1)}, bf16[512,128]{1,0:T(8,128)(2,1)S(1)}, u32[]{:S(2)}, u32[]{:S(2)}) collective-permute-start(bf16[512,128]{1,0:T(8,128)(2,1)S(1)} %get-tuple-element.21), channel_id=1, source_target_pairs={{496,0},{504,8},{0,16},{8,24},{16,32},{24,40},{32,48},{40,56},{48,... | collective-permute-start | bytes 393224 | tf_op jit(solution)/shard_map/ppermute | solution.py:34
  100.4 0.0 copy-start.5
  100.4 0.0 copy-start.6
  100.4 0.0 collective-permute-done.r0
  100.4 0.0 collective-permute-done.1.r1
  100.4 4.4 %collective-permute-done.2.r2 = bf16[512,128]{1,0:T(8,128)(2,1)S(1)} collective-permute-done((bf16[512,128]{1,0:T(8,128)(2,1)S(1)}, bf16[512,128]{1,0:T(8,128)(2,1)S(1)}, u32[]{:S(2)}, u32[]{:S(2)}) %collective-permute-start.2) | collective-permute-done | bytes 131104 | tf_op jit(solution)/shard_map/ppermute | solution.py:34
  104.8 3.3 %collective-permute-done.3.r3 = bf16[512,128]{1,0:T(8,128)(2,1)S(1)} collective-permute-done((bf16[512,128]{1,0:T(8,128)(2,1)S(1)}, bf16[512,128]{1,0:T(8,128)(2,1)S(1)}, u32[]{:S(2)}, u32[]{:S(2)}) %collective-permute-start.3) | collective-permute-done | bytes 131104 | tf_op jit(solution)/shard_map/ppermute | solution.py:34
  108.1 0.0 copy-done
  108.2 0.0 copy-done.1
  108.2 0.0 copy-done.4
  108.2 0.0 copy-done.5
  108.2 0.0 copy-done.6
  108.2 1.8 %shard_map.84 = f32[64,384]{1,0:T(8,128)S(1)} custom-call(bf16[512,384]{1,0:T(8,128)(2,1)S(1)} %get-tuple-element.15.x, bf16[512,128]{1,0:T(8,128)(2,1)S(1)} %collective-permute-done.r0, bf16[512,128]{1,0:T(8,128)(2,1)S(1)} %collective-permute-done.1.r1, bf16[512,128]{1,0:T(8,128)(2,1)S(1)} %collective-permute-done.2.r2, ...), custom_call_target="tpu_custom_call" | custom-call | flops 226492416 | bytes 2000000 | tf_op jit(solution)/shard_map/pallas_call | solution.py:234
  110.0 0.0 all-to-all-done.3.shares
  110.0 0.1 shard_map.86
  110.1 10.0 %all-gather.2 = bf16[128,384]{1,0:T(8,128)(2,1)S(1)} all-gather(bf16[64,384]{1,0:T(8,128)(2,1)S(1)} %get-tuple-element.24), channel_id=4, replica_groups=mesh['zl'=4,'y'=8,'c'=2,'zh'=2,'x'=4] {'zh'}, dimensions={0}, use_global_device_ids=true | all-gather | bytes 147456 | tf_op jit(solution)/shard_map/all_gather | solution.py:245
  120.0 0.6 fusion.1
  (1 shorter events, 0.0 us)
Async XLA Ops:
  12.3 10.3 %copy-start.2 = (bf16[3,512,64]{1,2,0:T(8,128)(2,1)S(1)}, bf16[3,512,64]{1,2,0:T(8,128)(2,1)}, u32[]{:S(2)}) copy-start(bf16[3,512,64]{1,2,0:T(8,128)(2,1)} %param.14) | copy-start | bytes 589828
  23.6 23.7 %all-to-all-start.1 = ((bf16[8,64,384]{2,1,0:T(8,128)(2,1)}), bf16[8,64,384]{2,1,0:T(8,128)(2,1)S(1)}, u32[]{:S(2)}, u32[]{:S(2)}) async-start(bf16[8,64,384]{2,1,0:T(8,128)(2,1)} %get-tuple-element.16), calls=%async_computation.1 | async-start | bytes 786432 | tf_op jit(solution)/shard_map/all_to_all | solution.py:204
  59.9 23.5 %copy-start.3 = (bf16[64,512]{1,0:T(8,128)(2,1)S(1)}, bf16[64,512]{1,0:T(8,128)(2,1)}, u32[]{:S(2)}) copy-start(bf16[64,512]{1,0:T(8,128)(2,1)} %w_out.1) | copy-start | bytes 196612
  84.5 23.6 %copy-start = (bf16[3,4,128,128]{3,2,1,0:T(8,128)(2,1)S(1)}, bf16[3,4,128,128]{3,2,1,0:T(8,128)(2,1)}, u32[]{:S(2)}) copy-start(bf16[3,4,128,128]{3,2,1,0:T(8,128)(2,1)} %tiles.1) | copy-start | bytes 1179652
  84.5 23.6 %copy-start.1 = (bf16[384,64]{0,1:T(8,128)(2,1)S(1)}, bf16[384,64]{0,1:T(8,128)(2,1)}, u32[]{:S(2)}) copy-start(bf16[384,64]{0,1:T(8,128)(2,1)} %param.8) | copy-start | bytes 147460
  84.5 23.6 %copy-start.4 = (bf16[512,64]{0,1:T(8,128)(2,1)S(1)}, bf16[512,64]{0,1:T(8,128)(2,1)}, u32[]{:S(2)}) copy-start(bf16[512,64]{0,1:T(8,128)(2,1)} %param.13) | copy-start | bytes 196612
  84.5 25.5 %all-to-all-start.3 = ((bf16[4,2,64,384]{3,2,1,0:T(8,128)(2,1)}), bf16[4,2,64,384]{3,2,1,0:T(8,128)(2,1)S(1)}, u32[]{:S(2)}, u32[]{:S(2)}) async-start(bf16[4,2,64,384]{3,2,1,0:T(8,128)(2,1)} %shard_map.85), calls=%async_computation.3 | async-start | bytes 786432 | tf_op jit(solution)/shard_map/all_to_all | solution.py:233
  90.2 10.2 %collective-permute-start = (bf16[512,128]{1,0:T(8,128)(2,1)S(1)}, bf16[512,128]{1,0:T(8,128)(2,1)S(1)}, u32[]{:S(2)}, u32[]{:S(2)}) collective-permute-start(bf16[512,128]{1,0:T(8,128)(2,1)S(1)} %get-tuple-element.18), channel_id=1, source_target_pairs={{16,0},{24,8},{32,16},{40,24},{48,32},{56,40},{64,48},{72,56},{80,... | collective-permute-start | bytes 393224 | tf_op jit(solution)/shard_map/ppermute | solution.py:34
  92.1 8.3 %collective-permute-start.1 = (bf16[512,128]{1,0:T(8,128)(2,1)S(1)}, bf16[512,128]{1,0:T(8,128)(2,1)S(1)}, u32[]{:S(2)}, u32[]{:S(2)}) collective-permute-start(bf16[512,128]{1,0:T(8,128)(2,1)S(1)} %get-tuple-element.19), channel_id=1, source_target_pairs={{8,0},{16,8},{24,16},{32,24},{40,32},{48,40},{56,48},{64,56},{72,6... | collective-permute-start | bytes 393224 | tf_op jit(solution)/shard_map/ppermute | solution.py:34
  94.6 10.2 %collective-permute-start.2 = (bf16[512,128]{1,0:T(8,128)(2,1)S(1)}, bf16[512,128]{1,0:T(8,128)(2,1)S(1)}, u32[]{:S(2)}, u32[]{:S(2)}) collective-permute-start(bf16[512,128]{1,0:T(8,128)(2,1)S(1)} %get-tuple-element.20), channel_id=1, source_target_pairs={{504,0},{0,8},{8,16},{16,24},{24,32},{32,40},{40,48},{48,56},{56,6... | collective-permute-start | bytes 393224 | tf_op jit(solution)/shard_map/ppermute | solution.py:34
  96.5 11.6 %collective-permute-start.3 = (bf16[512,128]{1,0:T(8,128)(2,1)S(1)}, bf16[512,128]{1,0:T(8,128)(2,1)S(1)}, u32[]{:S(2)}, u32[]{:S(2)}) collective-permute-start(bf16[512,128]{1,0:T(8,128)(2,1)S(1)} %get-tuple-element.21), channel_id=1, source_target_pairs={{496,0},{504,8},{0,16},{8,24},{16,32},{24,40},{32,48},{40,56},{48,... | collective-permute-start | bytes 393224 | tf_op jit(solution)/shard_map/ppermute | solution.py:34
  100.4 7.8 %copy-start.5 = (s32[3,4]{1,0:T(4,128)S(1)}, s32[3,4]{1,0:T(4,128)}, u32[]{:S(2)}) copy-start(s32[3,4]{1,0:T(4,128)} %cols.1) | copy-start | bytes 148
  100.4 7.8 %copy-start.6 = (s32[3]{0:T(128)S(1)}, s32[3]{0:T(128)}, u32[]{:S(2)}) copy-start(s32[3]{0:T(128)} %counts.1) | copy-start | bytes 40

commit v5 on v4

--- a/solution.py
+++ b/solution.py
@@ -136,7 +136,7 @@
         block[...] = matmul(x[...], spot.astype(jnp.bfloat16), ((1,), (0,))).astype(jnp.bfloat16)
 
 
-def combine_body(parts, w_out, out):
+def combine_body(parts, w_out, other, own, shares):
     count = parts.shape[0]
     tail = [parts[i, DH:, :].astype(jnp.float32) for i in range(count)]
     tops = [t[0:1] + t[1:2] + t[2:3] for t in tail]
@@ -151,20 +151,20 @@
         total = total + factor * sums[i]
         value = value + factor * parts[i, :DH, :].astype(jnp.float32)
     heads_out = (value / total).astype(jnp.bfloat16)
-    per_x, per_z = out.shape[:2]
+    per_z, per_x = shares.shape[:2]
     for z in range(per_z):
         for x in range(per_x):
             at = (z * per_x + x) * DH
             share = matmul(w_out[:, at : at + DH], heads_out, ((0,), (0,)))
-            out[x, z] = share.astype(jnp.bfloat16)
-
-
-def fold_body(shares, keep, send):
+            shares[z, x] = share.astype(jnp.bfloat16)
     mine = lax.axis_index("zh")
-    total = [shares[x, mine].astype(jnp.float32) for x in range(shares.shape[0])]
-    keep[...] = sum(total[1:], total[0])
-    total = [shares[x, 1 - mine].astype(jnp.float32) for x in range(shares.shape[0])]
-    send[...] = sum(total[1:], total[0]).astype(jnp.bfloat16)
+    other[...] = shares[1 - mine]
+    own[...] = shares[mine]
+
+
+def fold_body(shares, out):
+    total = [shares[x].astype(jnp.float32) for x in range(shares.shape[0])]
+    out[...] = sum(total[1:], total[0]).astype(out.dtype)
 
 
 def message_body(x, r0, r1, r2, r3, tiles, counts, cols, w_msg, own_x, out, table):
@@ -224,13 +224,15 @@
     )(queries, held, x_full, pltpu.with_memory_space_constraint(listed, pltpu.HBM))
     parts = lax.all_to_all(parts, "y", 0, 0)
     per_x, per_z = lax.axis_size("x"), lax.axis_size("zh")
-    shares = call(
-        combine_body, [((per_x, per_z, DH, rows), bf16)], count=2, flops=2 * D * DH * rows
+    other, own = call(
+        combine_body,
+        [((per_x, DH, rows), bf16)] * per_z,
+        scratch=[pltpu.VMEM((per_z, per_x, DH, rows), bf16)],
+        count=2,
+        flops=2 * D * DH * rows,
     )(parts, w_out)
-    received = []
-    for block, offset in zip(chosen, offsets(REACH)):
-        received.append(passed_along(block, DOM, offset))
-    shares = lax.all_to_all(shares, "x", 0, 0)
+    received = [passed_along(block, DOM, o) for block, o in zip(chosen, offsets(REACH))]
+    other = lax.all_to_all(other, "x", 0, 0)
     base = call(
         message_body,
         [((DH, rows), f32)],
@@ -239,10 +241,10 @@
         count=10,
         flops=2 * D * rows * (4 * bound + DH),
     )(x_full, *received, tile_vals, tile_counts, tile_cols, w_msg.T, x_own)
-    keep, send = call(
-        fold_body, [((DH, rows), f32), ((DH, rows), bf16)], count=1, flops=D * rows
-    )(shares)
+    send = call(fold_body, [((DH, rows), bf16)], count=1, flops=D * rows)(other)
+    own = lax.all_to_all(own, "x", 0, 0)
     halves = lax.all_gather(send, "zh", axis=0, tiled=False)
+    keep = own.astype(f32).sum(axis=0)
     others = jnp.where(lax.axis_index("zh") == 0, halves[1], halves[0])
     return (base + keep + others.astype(f32)).astype(bf16).T
 

time: 121 us -> 121 us (level)
  waiting for transfers between devices: 7.75 us -> 2.81 us
  starting transfers between devices: 22.6 us -> 27.5 us
    ppermute x4, waiting for transfers between devices: 7.74 us -> 2.8 us  [passed_along(): lax.ppermute(block, axis, [((i - distance) % size, i) for i in range(size)])]
    all_to_all x1 -> x2, starting transfers between devices: 5.63 us -> 10.5 us  [the longest x1 5.54 us: local(): other = lax.all_to_all(other, 'x', 0, 0)]
  transfers between devices with their start and end apart: 6 -> 7, of which waited for: 2 -> 1; matrix products, arithmetic and copies ran while one was open for 0% -> 0% of each run, Pallas kernels for 1% -> 2%
where the time goes in v5:
time: 121 us
  blocking collectives  72.8 us (60%)
  starting transfers between devices  27.5 us (23%)
  Pallas kernels  16.7 us (14%)
  waiting for transfers between devices  2.81 us (2%)
    all_to_all x1, blocking collectives, local(): parts = lax.all_to_all(parts, 'y', 0, 0)  23.5 us
    all_gather x1, blocking collectives, local(): held = lax.all_gather(kv, ('zl', 'c'), axis=0, tiled=False)  16.8 us
    pallas_call x1, Pallas kernels, local(): call(attend_body, [((askers, CARRY, rows), bf16)] + [((D, bound), bf16)]...  12.7 us
    all_gather x1, blocking collectives, local(): pair = lax.all_gather(x_own, 'zh', axis=0, tiled=False)  12.2 us
    all_to_all x1, blocking collectives, sent_to_all(): lax.all_to_all(jnp.broadcast_to(block, (size,) + block.shape), axis, 0, 0)  10.3 us
    ppermute x4, starting transfers between devices, passed_along(): lax.ppermute(block, axis, [((i - distance) % size, i) for i in range(size)])  10.2 us
    all_gather x1, blocking collectives, local(): halves = lax.all_gather(send, 'zh', axis=0, tiled=False)  9.96 us
    all_to_all x1, starting transfers between devices, local(): queries = lax.all_to_all(q, 'y', 0, 0)  6.83 us
  transfers between devices with their start and end apart: 7, of which 1 were waited for; matrix products, arithmetic and copies ran while one was open for 0% of the time, Pallas kernels for 2%

profile of v5, /device:TPU:6, one launch (start us, length us, event | category | flops | bytes accessed | tf_op | source)
XLA Modules:
  0.0 120.7 jit_solution(4997361562659601258)
XLA Ops:
  0.0 12.2 %all-gather = bf16[128,384]{1,0:T(8,128)(2,1)S(1)} all-gather(bf16[64,384]{1,0:T(8,128)(2,1)} %bitcast.11), channel_id=2, replica_groups=mesh['zl'=4,'y'=8,'c'=2,'zh'=2,'x'=4] {'zh'}, dimensions={0}, use_global_device_ids=true | all-gather | bytes 147456 | tf_op jit(solution)/shard_map/all_gather | solution.py:195
  12.3 0.0 copy-start.2
  12.3 10.3 %all_to_all.25.quad = bf16[4,2,64,384]{3,2,1,0:T(8,128)(2,1)S(1)} all-to-all(bf16[4,2,64,384]{3,2,1,0:T(8,128)(2,1)S(1)} %broadcast_in_dim.3), channel_id=1, replica_groups=mesh['zl'=4,'y'=8,'c'=2,'zh'=2,'x'=4] {'x'}, dimensions={0} | all-to-all | bytes 786432 | tf_op jit(solution)/shard_map/all_to_all | solution.py:39
  22.6 0.0 copy-done.2
  22.6 1.0 shard_map.82
  23.6 6.8 %all-to-all-start.1 = ((bf16[8,64,384]{2,1,0:T(8,128)(2,1)}), bf16[8,64,384]{2,1,0:T(8,128)(2,1)S(1)}, u32[]{:S(2)}, u32[]{:S(2)}) async-start(bf16[8,64,384]{2,1,0:T(8,128)(2,1)} %get-tuple-element.16), calls=%async_computation.1 | async-start | bytes 786432 | tf_op jit(solution)/shard_map/all_to_all | solution.py:204
  30.4 16.8 %all-gather.1 = bf16[1024,384]{1,0:T(8,128)(2,1)S(1)} all-gather(bf16[128,384]{1,0:T(8,128)(2,1)S(1)} %get-tuple-element.17), channel_id=3, replica_groups=mesh['zl'=4,'y'=8,'c'=2,'zh'=2,'x'=4] {'zl','c'}, dimensions={0}, use_global_device_ids=true | all-gather | bytes 884736 | tf_op jit(solution)/shard_map/all_gather | solution.py:205
  47.2 0.0 all-to-all-done.1.q
  47.2 12.7 %shard_map.83 = (bf16[8,72,384]{2,1,0:T(8,128)(2,1)S(1)}, bf16[512,128]{1,0:T(8,128)(2,1)S(1)}, bf16[512,128]{1,0:T(8,128)(2,1)S(1)}, bf16[512,128]{1,0:T(8,128)(2,1)S(1)}, bf16[512,128]{1,0:T(8,128)(2,1)S(1)}) custom-call(bf16[8,64,384]{2,1,0:T(8,128)(2,1)S(1)} %all-to-all-done.1.q, bf16[8,128,384]{2,1,0:T(8,128)(2,1)S(1)} %bitcast.10, ...), custom_call_target="tpu_custom_call" | custom-call | flops 2415919104 | bytes 2000000 | tf_op jit(solution)/shard_map/pallas_call | solution.py:206
  59.9 0.0 copy-start.4
  59.9 23.5 %all_to_all.26.parts = bf16[8,72,384]{2,1,0:T(8,128)(2,1)S(1)} all-to-all(bf16[8,72,384]{2,1,0:T(8,128)(2,1)S(1)} %get-tuple-element.22), channel_id=1, replica_groups=mesh['zl'=4,'y'=8,'c'=2,'zh'=2,'x'=4] {'y'}, dimensions={0} | all-to-all | bytes 884736 | tf_op jit(solution)/shard_map/all_to_all | solution.py:225
  83.4 0.0 copy-done.4
  83.4 1.2 shard_map.85
  84.6 0.0 copy-start
  84.6 5.5 %all-to-all-start.4 = ((bf16[4,64,384]{2,1,0:T(8,128)(2,1)}), bf16[4,64,384]{2,1,0:T(8,128)(2,1)S(1)}, u32[]{:S(2)}, u32[]{:S(2)}) async-start(bf16[4,64,384]{2,1,0:T(8,128)(2,1)} %get-tuple-element.24), calls=%async_computation.4 | async-start | bytes 393216 | tf_op jit(solution)/shard_map/all_to_all | solution.py:235
  90.1 1.9 %collective-permute-start = (bf16[512,128]{1,0:T(8,128)(2,1)S(1)}, bf16[512,128]{1,0:T(8,128)(2,1)S(1)}, u32[]{:S(2)}, u32[]{:S(2)}) collective-permute-start(bf16[512,128]{1,0:T(8,128)(2,1)S(1)} %get-tuple-element.18), channel_id=1, source_target_pairs={{16,0},{24,8},{32,16},{40,24},{48,32},{56,40},{64,48},{72,56},{80,... | collective-permute-start | bytes 393224 | tf_op jit(solution)/shard_map/ppermute | solution.py:34
  92.1 2.5 %collective-permute-start.1 = (bf16[512,128]{1,0:T(8,128)(2,1)S(1)}, bf16[512,128]{1,0:T(8,128)(2,1)S(1)}, u32[]{:S(2)}, u32[]{:S(2)}) collective-permute-start(bf16[512,128]{1,0:T(8,128)(2,1)S(1)} %get-tuple-element.19), channel_id=1, source_target_pairs={{8,0},{16,8},{24,16},{32,24},{40,32},{48,40},{56,48},{64,56},{72,6... | collective-permute-start | bytes 393224 | tf_op jit(solution)/shard_map/ppermute | solution.py:34
  94.6 1.9 %collective-permute-start.2 = (bf16[512,128]{1,0:T(8,128)(2,1)S(1)}, bf16[512,128]{1,0:T(8,128)(2,1)S(1)}, u32[]{:S(2)}, u32[]{:S(2)}) collective-permute-start(bf16[512,128]{1,0:T(8,128)(2,1)S(1)} %get-tuple-element.20), channel_id=1, source_target_pairs={{504,0},{0,8},{8,16},{16,24},{24,32},{32,40},{40,48},{48,56},{56,6... | collective-permute-start | bytes 393224 | tf_op jit(solution)/shard_map/ppermute | solution.py:34
  96.5 3.8 %collective-permute-start.3 = (bf16[512,128]{1,0:T(8,128)(2,1)S(1)}, bf16[512,128]{1,0:T(8,128)(2,1)S(1)}, u32[]{:S(2)}, u32[]{:S(2)}) collective-permute-start(bf16[512,128]{1,0:T(8,128)(2,1)S(1)} %get-tuple-element.21), channel_id=1, source_target_pairs={{496,0},{504,8},{0,16},{8,24},{16,32},{24,40},{32,48},{40,56},{48,... | collective-permute-start | bytes 393224 | tf_op jit(solution)/shard_map/ppermute | solution.py:34
  100.3 0.0 all-to-all-done.4.shares
  100.3 0.0 copy-start.1
  100.4 0.0 copy-start.3
  100.4 4.9 %all-to-all-start.3 = ((bf16[4,64,384]{2,1,0:T(8,128)(2,1)}), bf16[4,64,384]{2,1,0:T(8,128)(2,1)S(1)}, u32[]{:S(2)}, u32[]{:S(2)}) async-start(bf16[4,64,384]{2,1,0:T(8,128)(2,1)} %get-tuple-element.23), calls=%async_computation.3 | async-start | bytes 393216 | tf_op jit(solution)/shard_map/all_to_all | solution.py:245
  105.3 0.0 copy-start.5
  105.3 0.0 copy-start.6
  105.3 0.0 collective-permute-done.r0
  105.3 0.0 collective-permute-done.1.r1
  105.3 0.0 collective-permute-done.2.r2
  105.3 2.8 %collective-permute-done.3.r3 = bf16[512,128]{1,0:T(8,128)(2,1)S(1)} collective-permute-done((bf16[512,128]{1,0:T(8,128)(2,1)S(1)}, bf16[512,128]{1,0:T(8,128)(2,1)S(1)}, u32[]{:S(2)}, u32[]{:S(2)}) %collective-permute-start.3) | collective-permute-done | bytes 131104 | tf_op jit(solution)/shard_map/ppermute | solution.py:34
  108.1 0.0 copy-done
  108.1 0.0 copy-done.1
  108.1 0.0 copy-done.3
  108.1 0.0 copy-done.5
  108.2 0.0 copy-done.6
  108.2 1.8 %shard_map.84 = f32[64,384]{1,0:T(8,128)S(1)} custom-call(bf16[512,384]{1,0:T(8,128)(2,1)S(1)} %get-tuple-element.15.x, bf16[512,128]{1,0:T(8,128)(2,1)S(1)} %collective-permute-done.r0, bf16[512,128]{1,0:T(8,128)(2,1)S(1)} %collective-permute-done.1.r1, bf16[512,128]{1,0:T(8,128)(2,1)S(1)} %collective-permute-done.2.r2, ...), custom_call_target="tpu_custom_call" | custom-call | flops 226492416 | bytes 2000000 | tf_op jit(solution)/shard_map/pallas_call | solution.py:236
  110.0 10.0 %all-gather.2 = bf16[128,384]{1,0:T(8,128)(2,1)S(1)} all-gather(bf16[64,384]{1,0:T(8,128)(2,1)S(1)} %shard_map.86), channel_id=4, replica_groups=mesh['zl'=4,'y'=8,'c'=2,'zh'=2,'x'=4] {'zh'}, dimensions={0}, use_global_device_ids=true | all-gather | bytes 147456 | tf_op jit(solution)/shard_map/all_gather | solution.py:246
  120.0 0.0 all-to-all-done.3
  120.0 0.6 fusion.1
  (3 shorter events, 0.1 us)
Async XLA Ops:
  12.3 10.3 %copy-start.2 = (bf16[3,512,64]{1,2,0:T(8,128)(2,1)S(1)}, bf16[3,512,64]{1,2,0:T(8,128)(2,1)}, u32[]{:S(2)}) copy-start(bf16[3,512,64]{1,2,0:T(8,128)(2,1)} %param.14) | copy-start | bytes 589828
  23.6 23.7 %all-to-all-start.1 = ((bf16[8,64,384]{2,1,0:T(8,128)(2,1)}), bf16[8,64,384]{2,1,0:T(8,128)(2,1)S(1)}, u32[]{:S(2)}, u32[]{:S(2)}) async-start(bf16[8,64,384]{2,1,0:T(8,128)(2,1)} %get-tuple-element.16), calls=%async_computation.1 | async-start | bytes 786432 | tf_op jit(solution)/shard_map/all_to_all | solution.py:204
  59.9 23.5 %copy-start.4 = (bf16[64,512]{1,0:T(8,128)(2,1)S(1)}, bf16[64,512]{1,0:T(8,128)(2,1)}, u32[]{:S(2)}) copy-start(bf16[64,512]{1,0:T(8,128)(2,1)} %w_out.1) | copy-start | bytes 196612
  84.6 23.5 %copy-start = (bf16[3,4,128,128]{3,2,1,0:T(8,128)(2,1)S(1)}, bf16[3,4,128,128]{3,2,1,0:T(8,128)(2,1)}, u32[]{:S(2)}) copy-start(bf16[3,4,128,128]{3,2,1,0:T(8,128)(2,1)} %tiles.1) | copy-start | bytes 1179652
  84.6 15.7 %all-to-all-start.4 = ((bf16[4,64,384]{2,1,0:T(8,128)(2,1)}), bf16[4,64,384]{2,1,0:T(8,128)(2,1)S(1)}, u32[]{:S(2)}, u32[]{:S(2)}) async-start(bf16[4,64,384]{2,1,0:T(8,128)(2,1)} %get-tuple-element.24), calls=%async_computation.4 | async-start | bytes 393216 | tf_op jit(solution)/shard_map/all_to_all | solution.py:235
  90.1 15.2 %collective-permute-start = (bf16[512,128]{1,0:T(8,128)(2,1)S(1)}, bf16[512,128]{1,0:T(8,128)(2,1)S(1)}, u32[]{:S(2)}, u32[]{:S(2)}) collective-permute-start(bf16[512,128]{1,0:T(8,128)(2,1)S(1)} %get-tuple-element.18), channel_id=1, source_target_pairs={{16,0},{24,8},{32,16},{40,24},{48,32},{56,40},{64,48},{72,56},{80,... | collective-permute-start | bytes 393224 | tf_op jit(solution)/shard_map/ppermute | solution.py:34
  92.1 13.3 %collective-permute-start.1 = (bf16[512,128]{1,0:T(8,128)(2,1)S(1)}, bf16[512,128]{1,0:T(8,128)(2,1)S(1)}, u32[]{:S(2)}, u32[]{:S(2)}) collective-permute-start(bf16[512,128]{1,0:T(8,128)(2,1)S(1)} %get-tuple-element.19), channel_id=1, source_target_pairs={{8,0},{16,8},{24,16},{32,24},{40,32},{48,40},{56,48},{64,56},{72,6... | collective-permute-start | bytes 393224 | tf_op jit(solution)/shard_map/ppermute | solution.py:34
  94.6 10.7 %collective-permute-start.2 = (bf16[512,128]{1,0:T(8,128)(2,1)S(1)}, bf16[512,128]{1,0:T(8,128)(2,1)S(1)}, u32[]{:S(2)}, u32[]{:S(2)}) collective-permute-start(bf16[512,128]{1,0:T(8,128)(2,1)S(1)} %get-tuple-element.20), channel_id=1, source_target_pairs={{504,0},{0,8},{8,16},{16,24},{24,32},{32,40},{40,48},{48,56},{56,6... | collective-permute-start | bytes 393224 | tf_op jit(solution)/shard_map/ppermute | solution.py:34
  96.5 11.6 %collective-permute-start.3 = (bf16[512,128]{1,0:T(8,128)(2,1)S(1)}, bf16[512,128]{1,0:T(8,128)(2,1)S(1)}, u32[]{:S(2)}, u32[]{:S(2)}) collective-permute-start(bf16[512,128]{1,0:T(8,128)(2,1)S(1)} %get-tuple-element.21), channel_id=1, source_target_pairs={{496,0},{504,8},{0,16},{8,24},{16,32},{24,40},{32,48},{40,56},{48,... | collective-permute-start | bytes 393224 | tf_op jit(solution)/shard_map/ppermute | solution.py:34
  100.3 7.8 %copy-start.1 = (bf16[384,64]{0,1:T(8,128)(2,1)S(1)}, bf16[384,64]{0,1:T(8,128)(2,1)}, u32[]{:S(2)}) copy-start(bf16[384,64]{0,1:T(8,128)(2,1)} %param.8) | copy-start | bytes 147460
  100.4 7.8 %copy-start.3 = (bf16[512,64]{0,1:T(8,128)(2,1)S(1)}, bf16[512,64]{0,1:T(8,128)(2,1)}, u32[]{:S(2)}) copy-start(bf16[512,64]{0,1:T(8,128)(2,1)} %param.13) | copy-start | bytes 196612
  100.4 19.6 %all-to-all-start.3 = ((bf16[4,64,384]{2,1,0:T(8,128)(2,1)}), bf16[4,64,384]{2,1,0:T(8,128)(2,1)S(1)}, u32[]{:S(2)}, u32[]{:S(2)}) async-start(bf16[4,64,384]{2,1,0:T(8,128)(2,1)} %get-tuple-element.23), calls=%async_computation.3 | async-start | bytes 393216 | tf_op jit(solution)/shard_map/all_to_all | solution.py:245
  105.3 2.8 %copy-start.5 = (s32[3,4]{1,0:T(4,128)S(1)}, s32[3,4]{1,0:T(4,128)}, u32[]{:S(2)}) copy-start(s32[3,4]{1,0:T(4,128)} %cols.1) | copy-start | bytes 148
  105.3 2.8 %copy-start.6 = (s32[3]{0:T(128)S(1)}, s32[3]{0:T(128)}, u32[]{:S(2)}) copy-start(s32[3]{0:T(128)} %counts.1) | copy-start | bytes 40

commit v6 on v4

--- a/solution.py
+++ b/solution.py
@@ -19,6 +19,7 @@
 CARRY = DH + 8
 TILE_Q = 256
 TILE_K = 256
+RING = [0, 2, 4, 6, 7, 5, 3, 1]
 INTERPRET = False
 
 
@@ -202,7 +203,7 @@
         flops=2 * D * rows * 3 * DH,
     )(quad, weights)
     queries = lax.all_to_all(q, "y", 0, 0)
-    held = lax.all_gather(kv, ("zl", "c"), axis=0, tiled=False)
+    held = lax.all_gather(kv, ("zl", "c"), axis=0, tiled=False, axis_index_groups=[RING])
     parts, *chosen = call(
         attend_body,
         [((askers, CARRY, rows), bf16)] + [((D, bound), bf16)] * directions,
@@ -227,9 +228,7 @@
     shares = call(
         combine_body, [((per_x, per_z, DH, rows), bf16)], count=2, flops=2 * D * DH * rows
     )(parts, w_out)
-    received = []
-    for block, offset in zip(chosen, offsets(REACH)):
-        received.append(passed_along(block, DOM, offset))
+    received = [passed_along(block, DOM, o) for block, o in zip(chosen, offsets(REACH))]
     shares = lax.all_to_all(shares, "x", 0, 0)
     base = call(
         message_body,

time: 121 us -> 126 us (1.041)
  blocking collectives: 72.8 us -> 76.5 us
    all_gather x1, blocking collectives: 16.8 us -> 23.7 us  [local(): lax.all_gather(kv, ('zl', 'c'), axis=0, tiled=False, axis_index_groups=[R...]
    all_to_all x1, blocking collectives: 23.5 us -> 20.5 us  [local(): parts = lax.all_to_all(parts, 'y', 0, 0)]
where the time goes in v6:
time: 126 us
  blocking collectives  76.5 us (61%)
  starting transfers between devices  22.6 us (18%)
  Pallas kernels  16.7 us (13%)
  waiting for transfers between devices  8.86 us (7%)
    all_gather x1, blocking collectives, local(): lax.all_gather(kv, ('zl', 'c'), axis=0, tiled=False, axis_index_groups=[R...  23.7 us
    all_to_all x1, blocking collectives, local(): parts = lax.all_to_all(parts, 'y', 0, 0)  20.5 us
    pallas_call x1, Pallas kernels, local(): call(attend_body, [((askers, CARRY, rows), bf16)] + [((D, bound), bf16)]...  12.7 us
    all_gather x1, blocking collectives, local(): pair = lax.all_gather(x_own, 'zh', axis=0, tiled=False)  12.2 us
    all_to_all x1, blocking collectives, sent_to_all(): lax.all_to_all(jnp.broadcast_to(block, (size,) + block.shape), axis, 0, 0)  10.3 us
    ppermute x4, starting transfers between devices, passed_along(): lax.ppermute(block, axis, [((i - distance) % size, i) for i in range(size)])  10.2 us
    all_gather x1, blocking collectives, local(): halves = lax.all_gather(send, 'zh', axis=0, tiled=False)  9.72 us
    ppermute x4, waiting for transfers between devices, passed_along(): lax.ppermute(block, axis, [((i - distance) % size, i) for i in range(size)])  8.86 us
  transfers between devices with their start and end apart: 6, of which 2 were waited for; matrix products, arithmetic and copies ran while one was open for 0% of the time, Pallas kernels for 1%

profile of v6, /device:TPU:6, one launch (start us, length us, event | category | flops | bytes accessed | tf_op | source)
XLA Modules:
  0.0 125.5 jit_solution(1246555551564901797)
XLA Ops:
  0.0 12.2 %all-gather = bf16[128,384]{1,0:T(8,128)(2,1)S(1)} all-gather(bf16[64,384]{1,0:T(8,128)(2,1)} %bitcast.11), channel_id=2, replica_groups=mesh['zl'=4,'y'=8,'c'=2,'zh'=2,'x'=4] {'zh'}, dimensions={0}, use_global_device_ids=true | all-gather | bytes 147456 | tf_op jit(solution)/shard_map/all_gather | solution.py:196
  12.3 0.0 copy-start.2
  12.3 10.3 %all_to_all.20.quad = bf16[4,2,64,384]{3,2,1,0:T(8,128)(2,1)S(1)} all-to-all(bf16[4,2,64,384]{3,2,1,0:T(8,128)(2,1)S(1)} %broadcast_in_dim.3), channel_id=1, replica_groups=mesh['zl'=4,'y'=8,'c'=2,'zh'=2,'x'=4] {'x'}, dimensions={0} | all-to-all | bytes 786432 | tf_op jit(solution)/shard_map/all_to_all | solution.py:40
  22.6 0.0 copy-done.2
  22.6 1.0 shard_map.82
  23.6 6.8 %all-to-all-start.1 = ((bf16[8,64,384]{2,1,0:T(8,128)(2,1)}), bf16[8,64,384]{2,1,0:T(8,128)(2,1)S(1)}, u32[]{:S(2)}, u32[]{:S(2)}) async-start(bf16[8,64,384]{2,1,0:T(8,128)(2,1)} %get-tuple-element.16), calls=%async_computation.1 | async-start | bytes 786432 | tf_op jit(solution)/shard_map/all_to_all | solution.py:205
  30.4 23.7 %all-gather.1 = bf16[1024,384]{1,0:T(8,128)(2,1)S(1)} all-gather(bf16[128,384]{1,0:T(8,128)(2,1)S(1)} %get-tuple-element.17), channel_id=3, replica_groups={{0,128,256,384,392,264,136,8},{1,129,257,385,393,265,137,9},{2,130,258,..., dimensions={0}, use_global_device_ids=true | all-gather | bytes 884736 | tf_op jit(solution)/shard_map/all_gather | solution.py:206
  54.2 0.0 all-to-all-done.1.q
  54.2 12.7 %shard_map.83 = (bf16[8,72,384]{2,1,0:T(8,128)(2,1)S(1)}, bf16[512,128]{1,0:T(8,128)(2,1)S(1)}, bf16[512,128]{1,0:T(8,128)(2,1)S(1)}, bf16[512,128]{1,0:T(8,128)(2,1)S(1)}, bf16[512,128]{1,0:T(8,128)(2,1)S(1)}) custom-call(bf16[8,64,384]{2,1,0:T(8,128)(2,1)S(1)} %all-to-all-done.1.q, bf16[8,128,384]{2,1,0:T(8,128)(2,1)S(1)} %bitcast.10, ...), custom_call_target="tpu_custom_call" | custom-call | flops 2415919104 | bytes 2000000 | tf_op jit(solution)/shard_map/pallas_call | solution.py:207
  66.8 0.0 copy-start.3
  66.9 20.5 %all_to_all.21.parts = bf16[8,72,384]{2,1,0:T(8,128)(2,1)S(1)} all-to-all(bf16[8,72,384]{2,1,0:T(8,128)(2,1)S(1)} %get-tuple-element.22), channel_id=1, replica_groups=mesh['zl'=4,'y'=8,'c'=2,'zh'=2,'x'=4] {'y'}, dimensions={0} | all-to-all | bytes 884736 | tf_op jit(solution)/shard_map/all_to_all | solution.py:226
  87.4 0.0 copy-done.3
  87.4 1.1 shard_map.85
  88.5 0.0 copy-start
  88.5 0.0 copy-start.1
  88.5 0.0 copy-start.4
  88.5 5.6 %all-to-all-start.3 = ((bf16[4,2,64,384]{3,2,1,0:T(8,128)(2,1)}), bf16[4,2,64,384]{3,2,1,0:T(8,128)(2,1)S(1)}, u32[]{:S(2)}, u32[]{:S(2)}) async-start(bf16[4,2,64,384]{3,2,1,0:T(8,128)(2,1)} %shard_map.85), calls=%async_computation.3 | async-start | bytes 786432 | tf_op jit(solution)/shard_map/all_to_all | solution.py:232
  94.2 2.9 %collective-permute-start = (bf16[512,128]{1,0:T(8,128)(2,1)S(1)}, bf16[512,128]{1,0:T(8,128)(2,1)S(1)}, u32[]{:S(2)}, u32[]{:S(2)}) collective-permute-start(bf16[512,128]{1,0:T(8,128)(2,1)S(1)} %get-tuple-element.18), channel_id=1, source_target_pairs={{16,0},{24,8},{32,16},{40,24},{48,32},{56,40},{64,48},{72,56},{80,... | collective-permute-start | bytes 393224 | tf_op jit(solution)/shard_map/ppermute | solution.py:35
  97.1 2.5 %collective-permute-start.1 = (bf16[512,128]{1,0:T(8,128)(2,1)S(1)}, bf16[512,128]{1,0:T(8,128)(2,1)S(1)}, u32[]{:S(2)}, u32[]{:S(2)}) collective-permute-start(bf16[512,128]{1,0:T(8,128)(2,1)S(1)} %get-tuple-element.19), channel_id=1, source_target_pairs={{8,0},{16,8},{24,16},{32,24},{40,32},{48,40},{56,48},{64,56},{72,6... | collective-permute-start | bytes 393224 | tf_op jit(solution)/shard_map/ppermute | solution.py:35
  99.7 1.9 %collective-permute-start.2 = (bf16[512,128]{1,0:T(8,128)(2,1)S(1)}, bf16[512,128]{1,0:T(8,128)(2,1)S(1)}, u32[]{:S(2)}, u32[]{:S(2)}) collective-permute-start(bf16[512,128]{1,0:T(8,128)(2,1)S(1)} %get-tuple-element.20), channel_id=1, source_target_pairs={{504,0},{0,8},{8,16},{16,24},{24,32},{32,40},{40,48},{48,56},{56,6... | collective-permute-start | bytes 393224 | tf_op jit(solution)/shard_map/ppermute | solution.py:35
  101.6 2.8 %collective-permute-start.3 = (bf16[512,128]{1,0:T(8,128)(2,1)S(1)}, bf16[512,128]{1,0:T(8,128)(2,1)S(1)}, u32[]{:S(2)}, u32[]{:S(2)}) collective-permute-start(bf16[512,128]{1,0:T(8,128)(2,1)S(1)} %get-tuple-element.21), channel_id=1, source_target_pairs={{496,0},{504,8},{0,16},{8,24},{16,32},{24,40},{32,48},{40,56},{48,... | collective-permute-start | bytes 393224 | tf_op jit(solution)/shard_map/ppermute | solution.py:35
  104.4 0.0 copy-start.5
  104.4 0.0 copy-start.6
  104.4 0.0 collective-permute-done.r0
  104.4 0.0 collective-permute-done.1.r1
  104.4 5.4 %collective-permute-done.2.r2 = bf16[512,128]{1,0:T(8,128)(2,1)S(1)} collective-permute-done((bf16[512,128]{1,0:T(8,128)(2,1)S(1)}, bf16[512,128]{1,0:T(8,128)(2,1)S(1)}, u32[]{:S(2)}, u32[]{:S(2)}) %collective-permute-start.2) | collective-permute-done | bytes 131104 | tf_op jit(solution)/shard_map/ppermute | solution.py:35
  109.8 3.4 %collective-permute-done.3.r3 = bf16[512,128]{1,0:T(8,128)(2,1)S(1)} collective-permute-done((bf16[512,128]{1,0:T(8,128)(2,1)S(1)}, bf16[512,128]{1,0:T(8,128)(2,1)S(1)}, u32[]{:S(2)}, u32[]{:S(2)}) %collective-permute-start.3) | collective-permute-done | bytes 131104 | tf_op jit(solution)/shard_map/ppermute | solution.py:35
  113.3 0.0 copy-done
  113.3 0.0 copy-done.1
  113.3 0.0 copy-done.4
  113.3 0.0 copy-done.5
  113.3 0.0 copy-done.6
  113.3 1.8 %shard_map.84 = f32[64,384]{1,0:T(8,128)S(1)} custom-call(bf16[512,384]{1,0:T(8,128)(2,1)S(1)} %get-tuple-element.15.x, bf16[512,128]{1,0:T(8,128)(2,1)S(1)} %collective-permute-done.r0, bf16[512,128]{1,0:T(8,128)(2,1)S(1)} %collective-permute-done.1.r1, bf16[512,128]{1,0:T(8,128)(2,1)S(1)} %collective-permute-done.2.r2, ...), custom_call_target="tpu_custom_call" | custom-call | flops 226492416 | bytes 2000000 | tf_op jit(solution)/shard_map/pallas_call | solution.py:233
  115.1 0.0 all-to-all-done.3.shares
  115.1 0.1 shard_map.86
  115.2 9.7 %all-gather.2 = bf16[128,384]{1,0:T(8,128)(2,1)S(1)} all-gather(bf16[64,384]{1,0:T(8,128)(2,1)S(1)} %get-tuple-element.24), channel_id=4, replica_groups=mesh['zl'=4,'y'=8,'c'=2,'zh'=2,'x'=4] {'zh'}, dimensions={0}, use_global_device_ids=true | all-gather | bytes 147456 | tf_op jit(solution)/shard_map/all_gather | solution.py:244
  124.9 0.6 fusion.1
  (1 shorter events, 0.0 us)
Async XLA Ops:
  12.3 10.3 %copy-start.2 = (bf16[3,512,64]{1,2,0:T(8,128)(2,1)S(1)}, bf16[3,512,64]{1,2,0:T(8,128)(2,1)}, u32[]{:S(2)}) copy-start(bf16[3,512,64]{1,2,0:T(8,128)(2,1)} %param.14) | copy-start | bytes 589828
  23.6 30.6 %all-to-all-start.1 = ((bf16[8,64,384]{2,1,0:T(8,128)(2,1)}), bf16[8,64,384]{2,1,0:T(8,128)(2,1)S(1)}, u32[]{:S(2)}, u32[]{:S(2)}) async-start(bf16[8,64,384]{2,1,0:T(8,128)(2,1)} %get-tuple-element.16), calls=%async_computation.1 | async-start | bytes 786432 | tf_op jit(solution)/shard_map/all_to_all | solution.py:205
  66.8 20.6 %copy-start.3 = (bf16[64,512]{1,0:T(8,128)(2,1)S(1)}, bf16[64,512]{1,0:T(8,128)(2,1)}, u32[]{:S(2)}) copy-start(bf16[64,512]{1,0:T(8,128)(2,1)} %w_out.1) | copy-start | bytes 196612
  88.5 24.7 %copy-start = (bf16[3,4,128,128]{3,2,1,0:T(8,128)(2,1)S(1)}, bf16[3,4,128,128]{3,2,1,0:T(8,128)(2,1)}, u32[]{:S(2)}) copy-start(bf16[3,4,128,128]{3,2,1,0:T(8,128)(2,1)} %tiles.1) | copy-start | bytes 1179652
  88.5 24.7 %copy-start.1 = (bf16[384,64]{0,1:T(8,128)(2,1)S(1)}, bf16[384,64]{0,1:T(8,128)(2,1)}, u32[]{:S(2)}) copy-start(bf16[384,64]{0,1:T(8,128)(2,1)} %param.8) | copy-start | bytes 147460
  88.5 24.7 %copy-start.4 = (bf16[512,64]{0,1:T(8,128)(2,1)S(1)}, bf16[512,64]{0,1:T(8,128)(2,1)}, u32[]{:S(2)}) copy-start(bf16[512,64]{0,1:T(8,128)(2,1)} %param.13) | copy-start | bytes 196612
  88.5 26.6 %all-to-all-start.3 = ((bf16[4,2,64,384]{3,2,1,0:T(8,128)(2,1)}), bf16[4,2,64,384]{3,2,1,0:T(8,128)(2,1)S(1)}, u32[]{:S(2)}, u32[]{:S(2)}) async-start(bf16[4,2,64,384]{3,2,1,0:T(8,128)(2,1)} %shard_map.85), calls=%async_computation.3 | async-start | bytes 786432 | tf_op jit(solution)/shard_map/all_to_all | solution.py:232
  94.2 10.2 %collective-permute-start = (bf16[512,128]{1,0:T(8,128)(2,1)S(1)}, bf16[512,128]{1,0:T(8,128)(2,1)S(1)}, u32[]{:S(2)}, u32[]{:S(2)}) collective-permute-start(bf16[512,128]{1,0:T(8,128)(2,1)S(1)} %get-tuple-element.18), channel_id=1, source_target_pairs={{16,0},{24,8},{32,16},{40,24},{48,32},{56,40},{64,48},{72,56},{80,... | collective-permute-start | bytes 393224 | tf_op jit(solution)/shard_map/ppermute | solution.py:35
  97.1 7.3 %collective-permute-start.1 = (bf16[512,128]{1,0:T(8,128)(2,1)S(1)}, bf16[512,128]{1,0:T(8,128)(2,1)S(1)}, u32[]{:S(2)}, u32[]{:S(2)}) collective-permute-start(bf16[512,128]{1,0:T(8,128)(2,1)S(1)} %get-tuple-element.19), channel_id=1, source_target_pairs={{8,0},{16,8},{24,16},{32,24},{40,32},{48,40},{56,48},{64,56},{72,6... | collective-permute-start | bytes 393224 | tf_op jit(solution)/shard_map/ppermute | solution.py:35
  99.7 10.2 %collective-permute-start.2 = (bf16[512,128]{1,0:T(8,128)(2,1)S(1)}, bf16[512,128]{1,0:T(8,128)(2,1)S(1)}, u32[]{:S(2)}, u32[]{:S(2)}) collective-permute-start(bf16[512,128]{1,0:T(8,128)(2,1)S(1)} %get-tuple-element.20), channel_id=1, source_target_pairs={{504,0},{0,8},{8,16},{16,24},{24,32},{32,40},{40,48},{48,56},{56,6... | collective-permute-start | bytes 393224 | tf_op jit(solution)/shard_map/ppermute | solution.py:35
  101.6 11.7 %collective-permute-start.3 = (bf16[512,128]{1,0:T(8,128)(2,1)S(1)}, bf16[512,128]{1,0:T(8,128)(2,1)S(1)}, u32[]{:S(2)}, u32[]{:S(2)}) collective-permute-start(bf16[512,128]{1,0:T(8,128)(2,1)S(1)} %get-tuple-element.21), channel_id=1, source_target_pairs={{496,0},{504,8},{0,16},{8,24},{16,32},{24,40},{32,48},{40,56},{48,... | collective-permute-start | bytes 393224 | tf_op jit(solution)/shard_map/ppermute | solution.py:35
  104.4 8.9 %copy-start.5 = (s32[3,4]{1,0:T(4,128)S(1)}, s32[3,4]{1,0:T(4,128)}, u32[]{:S(2)}) copy-start(s32[3,4]{1,0:T(4,128)} %cols.1) | copy-start | bytes 148
  104.4 8.9 %copy-start.6 = (s32[3]{0:T(128)S(1)}, s32[3]{0:T(128)}, u32[]{:S(2)}) copy-start(s32[3]{0:T(128)} %counts.1) | copy-start | bytes 40
